TPU v7x, 128 devices: a whole 4x4x4 slice. The times are simulated.
128 devices in a mesh: row: 8 (over z, core), col: 16 (over x, y).
Axes of the slice: x: 4, y: 4, z: 4, core: 2. Of those that a mesh axis runs over, the one named last changes fastest.
Arguments:
- tokens: bfloat16 [2048, 8192], P('row', 'col'), may hold values from -6 to 6
- cotangent: bfloat16 [2048, 8192], P('row', 'col'), may hold values from -6 to 6
- gate_weight: bfloat16 [8192, 14336], P('row', 'col'), may hold values from -0.1875 to 0.1875
- up_weight: bfloat16 [8192, 14336], P('row', 'col'), may hold values from -0.1875 to 0.1875
- down_weight: bfloat16 [14336, 8192], P('col', 'row'), may hold values from -0.125 to 0.125
- tile_mask: int32 [64, 112], replicated, may hold values from 0 to 1, as said below
Outputs:
- output: bfloat16 [2048, 8192], P('row', 'col')
- input_grad: bfloat16 [2048, 8192], P('row', 'col')
- gate_grad: bfloat16 [8192, 14336], P('row', 'col')
- up_grad: bfloat16 [8192, 14336], P('row', 'col')
- down_grad: bfloat16 [14336, 8192], P('col', 'row')
Inputs may be any that keep to these rules, and one draw needn't show every extreme that they name: `tile_mask`: the mask is made of 8 x 16 blocks of 8 x 7 tiles (block (i, j) holds tile rows i * 8.. and tile columns j * 7..). Each block holds between 2 and 12 ones, some block exactly 12, and the whole mask exactly 896 ones.
All inputs are finite; a program needn't handle non-finite values.
Results may differ from a plain program's by a relative error of at most 0.013.
Values may be sent and summed in bfloat16 or wider, within the bound.
No kernel may reach another device: no remote copies, remote signals or barrier semaphores. Data moves between devices by JAX's collectives and lax.ppermute only.
A program may use at most 192 MiB of HBM per device.

v0:
```python
import jax
import jax.numpy as jnp
from jax import lax
from jax.experimental import pallas as pl
from jax.experimental.pallas import tpu as pltpu
from jax.sharding import PartitionSpec as P


BLK = 128
CAP = 12
UNROLL = 4
BF = jnp.bfloat16
F32 = jnp.float32
DIST = (0, 3, 1, 2)
MIB = 1 << 20


def shift(axis, k):
    perm = []
    for r in range(8):
        for c in range(16):
            at = {"z": r // 2, "core": r % 2, "x": c // 4, "y": c % 4}
            at[axis] = (at[axis] + k) % (2 if axis == "core" else 4)
            perm.append((r * 16 + c, (at["z"] * 2 + at["core"]) * 16 + at["x"] * 4 + at["y"]))
    return perm


def send(v, axis, k):
    return lax.ppermute(v, ("row", "col"), shift(axis, k))


def ring_gather(v, axis):
    h = v.shape[0] // 2
    a = send(v, axis, 1)
    b = send(v, axis, -1)
    c, d = a[:h], b[h:]
    return a, b, send(c, axis, 1), send(d, axis, -1)


def gather_four(v, axis):
    return [v, send(v, axis, 1), send(v, axis, -1), send(v, axis, 2)]


def scatter_four(parts, axis):
    own, minus, plus, far = parts
    return [own, send(minus, axis, -1), send(plus, axis, 1), send(far, axis, 2)]


def add(*vs):
    total = vs[0].astype(F32)
    for v in vs[1:]:
        total = total + v.astype(F32)
    return total.astype(BF)


def place(d):
    return jnp.where(d == 0, 0, jnp.where(d == 1, 2, jnp.where(d == 2, 3, 1)))


def pack_body(mask, where, gate, up, down, out, sems):
    row = where[0] * 2 + where[1]
    col = where[2] * 4 + where[3]

    def copies(slot, i, j):
        r = pl.ds(pl.multiple_of(i * BLK, BLK), BLK)
        c = pl.ds(pl.multiple_of(j * BLK, BLK), BLK)
        return (
            pltpu.make_async_copy(gate.at[r, c], out.at[slot, :, pl.ds(0, BLK)], sems.at[slot, 0]),
            pltpu.make_async_copy(up.at[r, c], out.at[slot, :, pl.ds(BLK, BLK)], sems.at[slot, 1]),
            pltpu.make_async_copy(
                down.at[c, r], out.at[slot, :, pl.ds(2 * BLK, BLK)], sems.at[slot, 2]
            ),
        )

    def tile_row(i, n):
        for j in range(7):
            m = mask[row * 8 + i, col * 7 + j]

            @pl.when((m != 0) & (n < CAP))
            def _(n=n, j=j):
                for copy in copies(n, i, j):
                    copy.start()

            n = n + m
        return n

    n = lax.fori_loop(0, 8, tile_row, jnp.int32(0))

    def finish(s, _):
        for copy in copies(s, 0, 0):
            copy.wait()
        return 0

    lax.fori_loop(0, jnp.minimum(n, CAP), finish, 0)


def pack(mask, where, gate, up, down):
    smem = pl.BlockSpec(memory_space=pltpu.SMEM)
    hbm = pl.BlockSpec(memory_space=pl.ANY)
    return pl.pallas_call(
        pack_body,
        out_shape=jax.ShapeDtypeStruct((CAP, BLK, 3 * BLK), BF),
        in_specs=[smem, smem, hbm, hbm, hbm],
        out_specs=pl.BlockSpec(memory_space=pltpu.VMEM),
        scratch_shapes=[pltpu.SemaphoreType.DMA((CAP, 3))],
        name="pack",
    )(mask, where, gate, up, down)


def plan_body(mask, where, table):
    z, core, x, y = where[0], where[1], where[2], where[3]
    col = x * 4 + y
    total = jnp.int32(0)
    for q in range(8):
        group = ((z + DIST[q % 4]) & 3) * 2 + (core ^ (q // 4))

        def tile_row(i, carry, q=q, group=group):
            total, slot = carry
            owner = group * 2 + i // 4
            sub = i % 4
            px = place((owner // 4 - x) & 3)
            py = place((owner % 4 - y) & 3)
            at_x_y = (py * 4 + px) * 4 + sub
            at_y_x = (px * 4 + py) * 4 + sub
            for j in range(7):
                m = mask[group * 8 + i, col * 7 + j]
                table[0, total] = slot
                table[1, total] = at_x_y
                table[2, total] = at_y_x
                table[3, total] = j
                slot = slot + m
                total = total + m
            return total, slot

        total, _ = lax.fori_loop(0, 8, tile_row, (total, jnp.int32(q * CAP)))
    for k in range(UNROLL):
        table[0, total + k] = 8 * CAP
        table[1, total + k] = 0
        table[2, total + k] = 0
        table[3, total + k] = 0
    table[4, 0] = (total + (UNROLL - 1)) // UNROLL


def plan(mask, where):
    smem = pl.BlockSpec(memory_space=pltpu.SMEM)
    return pl.pallas_call(
        plan_body,
        out_shape=jax.ShapeDtypeStruct((8, 128), jnp.int32),
        in_specs=[smem, smem],
        out_specs=smem,
        name="plan",
    )(mask, where)


NT = (((1,), (1,)), ((), ()))
TN = (((0,), (0,)), ((), ()))


def fetch(parts, buffer, sems, first):
    copies = []
    at = 0
    for ref in parts:
        n = ref.shape[0]
        copies.append(pltpu.make_async_copy(ref, buffer.at[pl.ds(at, n)], sems.at[first + len(copies)]))
        at += n
    for copy in copies:
        copy.start()
    return copies


def store(parts, buffer, sems, first):
    copies = []
    at = 0
    for ref in parts:
        n = ref.shape[0]
        copies.append(pltpu.make_async_copy(buffer.at[pl.ds(at, n)], ref, sems.at[first + len(copies)]))
        at += n
    for copy in copies:
        copy.start()
    return copies


def wait(copies):
    for copy in copies:
        copy.wait()


def clear(ref):
    def body(p, _):
        ref[p] = jnp.zeros(ref.shape[1:], ref.dtype)
        return 0

    lax.fori_loop(0, ref.shape[0], body, 0)


def settle(rows, sums):
    def body(p, _):
        sums[p] = rows[p].astype(BF)
        return 0

    lax.fori_loop(0, 64, body, 0)


def forward_body(table, *refs):
    token_parts, refs = refs[:4], refs[4:]
    weight_parts, refs = refs[:10], refs[10:]
    outs, refs = refs[:4], refs[4:]
    gu, hidden, acts, weights, rows, sums, sems = refs
    loads = fetch(token_parts, acts, sems, 0) + fetch(weight_parts, weights, sems, 4)
    weights[8 * CAP] = jnp.zeros((BLK, 3 * BLK), BF)
    clear(gu)
    clear(rows)
    wait(loads)
    steps = table[4, 0]

    def entry(k):
        return table[0, k], table[1, k], table[3, k]

    def forward(i, _):
        es = [entry(i * UNROLL + k) for k in range(UNROLL)]
        ds = [
            jnp.dot(acts[t], weights[s, :, : 2 * BLK], preferred_element_type=F32)
            for s, t, _ in es
        ]
        for (_, _, c), d in zip(es, ds):
            gu[c] += d
        return 0

    lax.fori_loop(0, steps, forward, 0)

    def activate(c, _):
        g = gu[c, :, :BLK]
        hidden[c] = (g * jax.nn.sigmoid(g) * gu[c, :, BLK:]).astype(BF)
        return 0

    lax.fori_loop(0, 7, activate, 0)

    def output(i, _):
        es = [entry(i * UNROLL + k) for k in range(UNROLL)]
        ds = [
            jnp.dot(hidden[c], weights[s, :, 2 * BLK :], preferred_element_type=F32)
            for s, _, c in es
        ]
        for (_, t, _), d in zip(es, ds):
            rows[t] += d
        return 0

    lax.fori_loop(0, steps, output, 0)
    settle(rows, sums)
    wait(store(outs, sums, sems, 0))


SMEM = pl.BlockSpec(memory_space=pltpu.SMEM)
HBM = pl.BlockSpec(memory_space=pl.ANY)
IN_VMEM = pl.BlockSpec(memory_space=pltpu.VMEM)


def cost(tiles, moved):
    return pl.CostEstimate(
        flops=tiles * 8 * 2 * 256 * BLK * BLK, bytes_accessed=moved, transcendentals=0
    )


def part_shapes(*tail):
    return [jax.ShapeDtypeStruct((16, *tail), BF)] * 4


def forward_work(table, token_parts, weight_parts):
    vmem = pltpu.VMEM
    return pl.pallas_call(
        forward_body,
        out_shape=part_shapes(256, BLK)
        + [jax.ShapeDtypeStruct((7, 256, 2 * BLK), F32), jax.ShapeDtypeStruct((7, 256, BLK), BF)],
        in_specs=[SMEM] + [HBM] * 14,
        out_specs=[HBM] * 4 + [IN_VMEM] * 2,
        scratch_shapes=[
            vmem((64, 256, BLK), BF),
            vmem((8 * CAP + 1, BLK, 3 * BLK), BF),
            vmem((64, 256, BLK), F32),
            vmem((64, 256, BLK), BF),
            pltpu.SemaphoreType.DMA((14,)),
        ],
        compiler_params=pltpu.CompilerParams(vmem_limit_bytes=36 * MIB),
        cost_estimate=cost(56 * 3 * 4, 20 * MIB),
        name="forward",
    )(table, *token_parts, *weight_parts)


def input_body(table, gu, hidden, *refs):
    cot_parts, refs = refs[:4], refs[4:]
    weight_parts, refs = refs[:10], refs[10:]
    outs, refs = refs[:4], refs[4:]
    grads, refs = refs[:5], refs[5:]
    gucot, cots, weights, hgrad, rows, sums, gsum, sems = refs
    loads = fetch(cot_parts, cots, sems, 0) + fetch(weight_parts, weights, sems, 4)
    weights[8 * CAP] = jnp.zeros((BLK, 3 * BLK), BF)
    clear(hgrad)
    clear(rows)
    wait(loads)
    steps = table[4, 0]

    def entry(k):
        return table[0, k], table[2, k], table[3, k]

    def middle(i, _):
        es = [entry(i * UNROLL + k) for k in range(UNROLL)]
        res = []
        for s, t, c in es:
            g = cots[t]
            res.append(
                (
                    lax.dot_general(g, weights[s, :, 2 * BLK :], NT, preferred_element_type=F32),
                    lax.dot_general(hidden[c], g, TN, preferred_element_type=F32),
                )
            )
        for (s, _, c), (hg, dg) in zip(es, res):
            hgrad[c] += hg
            gsum[s] = dg.astype(BF)
        return 0

    lax.fori_loop(0, steps, middle, 0)
    stores = store(grads, gsum, sems, 0)

    def cotangents(c, _):
        g = gu[c, :, :BLK]
        s = jax.nn.sigmoid(g)
        hg = hgrad[c]
        gucot[c, :, :BLK] = (hg * gu[c, :, BLK:] * s * (1.0 + g * (1.0 - s))).astype(BF)
        gucot[c, :, BLK:] = (hg * (g * s)).astype(BF)
        return 0

    lax.fori_loop(0, 7, cotangents, 0)

    def backward(i, _):
        es = [entry(i * UNROLL + k) for k in range(UNROLL)]
        res = [
            lax.dot_general(gucot[c], weights[s, :, : 2 * BLK], NT, preferred_element_type=F32)
            for s, _, c in es
        ]
        for (_, t, _), r in zip(es, res):
            rows[t] += r
        return 0

    lax.fori_loop(0, steps, backward, 0)
    settle(rows, sums)
    wait(stores + store(outs, sums, sems, 5))


def grad_shapes(width):
    return [jax.ShapeDtypeStruct((n, BLK, width), BF) for n in (12, 12, 12, 12, 48)]


def input_work(table, gu, hidden, cot_parts, weight_parts):
    vmem = pltpu.VMEM
    return pl.pallas_call(
        input_body,
        out_shape=part_shapes(256, BLK)
        + grad_shapes(BLK)
        + [jax.ShapeDtypeStruct((7, 256, 2 * BLK), BF)],
        in_specs=[SMEM] + [IN_VMEM] * 2 + [HBM] * 14,
        out_specs=[HBM] * 9 + [IN_VMEM],
        scratch_shapes=[
            vmem((64, 256, BLK), BF),
            vmem((8 * CAP + 1, BLK, 3 * BLK), BF),
            vmem((7, 256, BLK), F32),
            vmem((64, 256, BLK), F32),
            vmem((64, 256, BLK), BF),
            vmem((8 * CAP + 1, BLK, BLK), BF),
            pltpu.SemaphoreType.DMA((14,)),
        ],
        compiler_params=pltpu.CompilerParams(vmem_limit_bytes=44 * MIB),
        cost_estimate=cost(56 * 4 * 4, 22 * MIB),
        name="inputs",
    )(table, gu, hidden, *cot_parts, *weight_parts)


def grad_body(table, gucot, *refs):
    token_parts, refs = refs[:4], refs[4:]
    grads, refs = refs[:5], refs[5:]
    acts, gsum, sems = refs
    wait(fetch(token_parts, acts, sems, 0))
    steps = table[4, 0]

    def backward(i, _):
        es = [
            (table[0, i * UNROLL + k], table[1, i * UNROLL + k], table[3, i * UNROLL + k])
            for k in range(UNROLL)
        ]
        res = [
            lax.dot_general(acts[t], gucot[c], TN, preferred_element_type=F32) for _, t, c in es
        ]
        for (s, _, _), r in zip(es, res):
            gsum[s] = r.astype(BF)
        return 0

    lax.fori_loop(0, steps, backward, 0)
    wait(store(grads, gsum, sems, 0))


def grad_work(table, gucot, token_parts):
    vmem = pltpu.VMEM
    return pl.pallas_call(
        grad_body,
        out_shape=grad_shapes(2 * BLK),
        in_specs=[SMEM, IN_VMEM] + [HBM] * 4,
        out_specs=[HBM] * 5,
        scratch_shapes=[
            vmem((64, 256, BLK), BF),
            vmem((8 * CAP + 1, BLK, 2 * BLK), BF),
            pltpu.SemaphoreType.DMA((5,)),
        ],
        compiler_params=pltpu.CompilerParams(vmem_limit_bytes=20 * MIB),
        cost_estimate=cost(56 * 2 * 4, 10 * MIB),
        name="grads",
    )(table, gucot, *token_parts)


def zero_body(*outs):
    for out in outs:
        out[...] = jnp.zeros(out.shape, BF)


def zeros(*shapes):
    return pl.pallas_call(
        zero_body,
        out_shape=[jax.ShapeDtypeStruct(s, BF) for s in shapes],
        name="zeros",
    )()


def unpack_body(mask, where, *refs):
    downs, refs = refs[:4], refs[4:]
    pairs, refs = refs[:4], refs[4:]
    gate, up, down, total, sems = refs[3:]
    row = where[0] * 2 + where[1]
    col = where[2] * 4 + where[3]
    for s in range(CAP):
        for parts, lanes in ((pairs, slice(0, 2 * BLK)), (downs, slice(2 * BLK, 3 * BLK))):
            v = parts[0][s].astype(F32)
            for part in parts[1:]:
                v = v + part[s].astype(F32)
            total[s, :, lanes] = v.astype(BF)

    def copies(slot, i, j):
        r = pl.ds(pl.multiple_of(i * BLK, BLK), BLK)
        c = pl.ds(pl.multiple_of(j * BLK, BLK), BLK)
        return (
            pltpu.make_async_copy(total.at[slot, :, pl.ds(0, BLK)], gate.at[r, c], sems.at[slot, 0]),
            pltpu.make_async_copy(total.at[slot, :, pl.ds(BLK, BLK)], up.at[r, c], sems.at[slot, 1]),
            pltpu.make_async_copy(
                total.at[slot, :, pl.ds(2 * BLK, BLK)], down.at[c, r], sems.at[slot, 2]
            ),
        )

    def tile_row(i, n):
        for j in range(7):
            m = mask[row * 8 + i, col * 7 + j]

            @pl.when((m != 0) & (n < CAP))
            def _(n=n, j=j):
                for copy in copies(n, i, j):
                    copy.start()

            n = n + m
        return n

    n = lax.fori_loop(0, 8, tile_row, jnp.int32(0))

    def finish(s, _):
        for copy in copies(s, 0, 0):
            copy.wait()
        return 0

    lax.fori_loop(0, jnp.minimum(n, CAP), finish, 0)


def unpack(mask, where, downs, pairs, blanks):
    return pl.pallas_call(
        unpack_body,
        out_shape=[jax.ShapeDtypeStruct(v.shape, BF) for v in blanks],
        in_specs=[SMEM, SMEM] + [IN_VMEM] * 8 + [HBM] * 3,
        out_specs=[HBM, HBM, HBM],
        scratch_shapes=[
            pltpu.VMEM((CAP, BLK, 3 * BLK), BF),
            pltpu.SemaphoreType.DMA((CAP, 3)),
        ],
        input_output_aliases={10: 0, 11: 1, 12: 2},
        name="unpack",
    )(mask, where, *downs, *pairs, *blanks)


def on_device(tokens, cotangent, gate_weight, up_weight, down_weight, tile_mask):
    row = lax.axis_index("row")
    col = lax.axis_index("col")
    where = jnp.stack([row // 2, row % 2, col // 4, col % 4]).astype(jnp.int32)

    packed = pack(tile_mask, where, gate_weight, up_weight, down_weight)
    table = plan(tile_mask, where)

    def gather(v, first, second):
        own = jnp.stack([v[:, k * BLK : k * BLK + BLK] for k in range(4)], 0)
        line = jnp.concatenate(gather_four(own, first), 0)
        return gather_four(line, second)

    def finish(got, axis):
        line = [add(*(v[k * 4 : k * 4 + 4] for v in got)) for k in range(4)]
        end = add(*scatter_four(line, axis))
        return jnp.concatenate([end[k] for k in range(4)], 1)

    def row_sums(grads):
        pair = send(grads[4], "core", 1)
        return [add(v, pair[k * CAP : k * CAP + CAP]) for k, v in enumerate(grads[:4])]

    token_parts = gather(tokens, "x", "y")
    a, b, c, d = ring_gather(packed, "z")
    mine = [packed, a, b, c, d]
    weight_parts = mine + [send(v, "core", 1) for v in mine]
    cot_parts = gather(cotangent, "y", "x")

    *outs, gu, hidden = forward_work(table, token_parts, weight_parts)
    outs = scatter_four(outs, "y")
    res = input_work(table, gu, hidden, cot_parts, weight_parts)
    ins, downs, gucot = res[:4], res[4:9], res[9]
    ins = scatter_four(ins, "x")
    downs = scatter_four(row_sums(downs), "z")
    pairs = grad_work(table, gucot, token_parts)
    pairs = scatter_four(row_sums(pairs), "z")
    output = finish(outs, "x")
    blanks = zeros(gate_weight.shape, up_weight.shape, down_weight.shape)
    gate_grad, up_grad, down_grad = unpack(tile_mask, where, downs, pairs, blanks)
    input_grad = finish(ins, "y")
    return output, input_grad, gate_grad, up_grad, down_grad


def solution(mesh):
    spec = P("row", "col")
    turned = P("col", "row")

    return jax.shard_map(
        on_device,
        mesh=mesh,
        in_specs=(spec, spec, spec, spec, turned, P()),
        out_specs=(spec, spec, spec, spec, turned),
        check_vma=False,
    )
```

profile of v0, /device:TPU:0, one launch (start us, length us, event | category | flops | bytes accessed | tf_op | source)
XLA Modules:
  0.0 327.0 jit_solution(7426442920950562890)
XLA Ops:
  0.6 1.0 slice_bitcast_fusion.15
  2.3 1.6 collective-permute-start
  3.9 1.6 collective-permute-start.1
  5.6 1.9 collective-permute-start.2
  8.2 3.9 %pack.1.refs_4_ = bf16[12,128,384]{2,1,0:T(8,128)(2,1)} custom-call(s32[64,112]{1,0:T(8,128)} %mask.5, s32[4]{0:T(128)} %pad_add_fusion.where, bf16[1024,896]{1,0:T(8,128)(2,1)} %gate.1, bf16[1024,896]{1,0:T(8,128)(2,1)} %up.1, bf16[896,1024]{1,0:T(8,128)(2,1)} %down.1), custom_call_target="tpu_custom_call" | custom-call | tf_op jit(solution)/shard_map/pack/pallas_call | solution.py:100
  12.1 2.0 collective-permute-start.6
  14.1 2.2 collective-permute-start.7
  18.8 1.0 slice_bitcast_fusion.11
  20.7 1.3 collective-permute-start.21
  22.0 1.0 constant_dynamic-update-slice_fusion.2
  23.1 1.0 constant_dynamic-update-slice_fusion.1
  24.1 1.0 constant_dynamic-update-slice_fusion.refs_0_
  25.1 2.1 collective-permute-start.3
  27.2 1.6 collective-permute-done.21
  28.9 1.9 collective-permute-start.4
  30.8 10.7 %collective-permute-done.6.refs_5_ = bf16[12,128,384]{2,1,0:T(8,128)(2,1)S(1)} collective-permute-done((bf16[12,128,384]{2,1,0:T(8,128)(2,1)}, bf16[12,128,384]{2,1,0:T(8,128)(2,1)S(1)}, u32[]{:S(2)}, u32[]{:S(2)}) %collective-permute-start.6) | collective-permute-done | bytes 1179680 | tf_op jit(solution)/shard_map/ppermute | solution.py:29
  41.5 2.9 collective-permute-start.22
  45.3 1.1 slice.233
  46.4 14.1 %collective-permute-done.22 = bf16[4,256,128]{2,1,0:T(8,128)(2,1)S(1)} collective-permute-done((bf16[4,256,128]{2,1,0:T(8,128)(2,1)S(1)}, bf16[4,256,128]{2,1,0:T(8,128)(2,1)S(1)}, u32[]{:S(2)}, u32[]{:S(2)}) %collective-permute-start.22) | collective-permute-done | bytes 262176 | tf_op jit(solution)/shard_map/ppermute | solution.py:29
  60.6 3.2 collective-permute-start.9
  63.8 1.0 copy-done.18
  64.8 1.9 collective-permute-start.5
  66.7 1.0 copy-done.20
  67.7 1.0 copy-done.23
  70.4 2.0 collective-permute-done.8.refs_7_
  73.9 5.9 %plan.1.table = s32[8,128]{1,0:T(8,128)} custom-call(s32[64,112]{1,0:T(8,128)} %mask.5, s32[4]{0:T(128)} %pad_add_fusion.where), custom_call_target="tpu_custom_call" | custom-call | tf_op jit(solution)/shard_map/plan/pallas_call | solution.py:146
  79.9 1.6 constant_dynamic-update-slice_fusion.10
  81.5 1.7 constant_dynamic-update-slice_fusion.9
  83.1 1.7 constant_dynamic-update-slice_fusion.8
  84.8 1.7 constant_dynamic-update-slice_fusion.7.refs_0_
  86.8 1.0 collective-permute-start.24
  87.8 2.3 collective-permute-start.25
  90.7 1.2 copy-done.16
  91.9 1.2 copy-done.21
  93.1 1.2 copy-done.24
  94.3 15.8 %forward.1 = (bf16[16,256,128]{2,1,0:T(8,128)(2,1)S(1)}, bf16[16,256,128]{2,1,0:T(8,128)(2,1)S(1)}, bf16[16,256,128]{2,1,0:T(8,128)(2,1)S(1)}, bf16[16,256,128]{...) custom-call(s32[8,128]{1,0:T(8,128)S(1)} %copy-done.14, ...), custom_call_target="tpu_custom_call" | custom-call | flops 45097156608 | bytes 20971520 | tf_op jit(solution)/shard_map/forward/pallas_call | solution.py:270
  110.1 25.8 %collective-permute-done.24.refs_1_ = bf16[16,256,128]{2,1,0:T(8,128)(2,1)S(1)} collective-permute-done((bf16[16,256,128]{2,1,0:T(8,128)(2,1)}, bf16[16,256,128]{2,1,0:T(8,128)(2,1)S(1)}, u32[]{:S(2)}, u32[]{:S(2)}) %collective-permute-start.24) | collective-permute-done | bytes 1048608 | tf_op jit(solution)/shard_map/ppermute | solution.py:29
  136.0 1.0 copy-done.39
  137.6 21.2 %inputs.1 = (bf16[16,256,128]{2,1,0:T(8,128)(2,1)S(1)}, bf16[16,256,128]{2,1,0:T(8,128)(2,1)}, bf16[16,256,128]{2,1,0:T(8,128)(2,1)}, bf16[16,256,128]{2,1,0:T(8...) custom-call(s32[8,128]{1,0:T(8,128)S(1)} %copy-done.14, ...), custom_call_target="tpu_custom_call" | custom-call | flops 60129542144 | bytes 23068672 | tf_op jit(solution)/shard_map/inputs/pallas_call | solution.py:355
  158.8 8.8 %grads.1 = (bf16[12,128,256]{2,1,0:T(8,128)(2,1)S(1)}, bf16[12,128,256]{2,1,0:T(8,128)(2,1)S(1)}, bf16[12,128,256]{2,1,0:T(8,128)(2,1)S(1)}, bf16[12,128,256]{2,1,0:T(8,128)(2,1)S(1)}, bf16[48,128,256]{2,1,0:T(8,128)(2,1)}) custom-call(s32[8,128]{1,0:T(8,128)S(1)} %copy-done.14, bf16[7,256,256]{2,1,0:T(8,128)(2,1)S(1)} %get-tuple-element.47.gucot, ...), custom_call_target="tpu_custom_call" | custom-call | flops 30064771072 | bytes 10485760 | tf_op jit(solution)/shard_map/grads/pallas_call | solution.py:402
  168.5 0.9 copy-done.3
  169.4 0.9 copy-done.5
  170.3 1.6 collective-permute-start.17
  171.9 4.5 %collective-permute-start.16 = (bf16[16,256,128]{2,1,0:T(8,128)(2,1)S(1)}, bf16[16,256,128]{2,1,0:T(8,128)(2,1)S(1)}, u32[]{:S(2)}, u32[]{:S(2)}) collective-permute-start(bf16[16,256,128]{2,1,0:T(8,128)(2,1)S(1)} %get-tuple-element.34), channel_id=1, source_target_pairs={{0,1},{1,2},{2,3},{3,0},{4,5},{5,6},{6,7},{7,4},{8,9},{9,10},{10,1... | collective-permute-start | bytes 3145736 | tf_op jit(solution)/shard_map/ppermute | solution.py:29
  176.7 21.2 %collective-permute-done.17 = bf16[16,256,128]{2,1,0:T(8,128)(2,1)S(1)} collective-permute-done((bf16[16,256,128]{2,1,0:T(8,128)(2,1)S(1)}, bf16[16,256,128]{2,1,0:T(8,128)(2,1)S(1)}, u32[]{:S(2)}, u32[]{:S(2)}) %collective-permute-start.17) | collective-permute-done | bytes 1048608 | tf_op jit(solution)/shard_map/ppermute | solution.py:29
  197.9 22.0 %collective-permute-done.16 = bf16[16,256,128]{2,1,0:T(8,128)(2,1)S(1)} collective-permute-done((bf16[16,256,128]{2,1,0:T(8,128)(2,1)S(1)}, bf16[16,256,128]{2,1,0:T(8,128)(2,1)S(1)}, u32[]{:S(2)}, u32[]{:S(2)}) %collective-permute-start.16) | collective-permute-done | bytes 1048608 | tf_op jit(solution)/shard_map/ppermute | solution.py:29
  220.0 2.6 collective-permute-done.15
  222.5 1.0 copy-done.29
  223.5 2.6 zeros.1
  226.1 2.0 add_convert_fusion.16
  228.3 17.9 %collective-permute-done.27 = bf16[16,256,128]{2,1,0:T(8,128)(2,1)} collective-permute-done((bf16[16,256,128]{2,1,0:T(8,128)(2,1)}, bf16[16,256,128]{2,1,0:T(8,128)(2,1)}, u32[]{:S(2)}, u32[]{:S(2)}) %collective-permute-start.27) | collective-permute-done | bytes 1048608 | tf_op jit(solution)/shard_map/ppermute | solution.py:29
  247.0 2.0 add_convert_fusion.11
  249.0 8.5 %collective-permute-start.32 = (bf16[4,256,128]{2,1,0:T(8,128)(2,1)S(1)}, bf16[4,256,128]{2,1,0:T(8,128)(2,1)S(1)}, u32[]{:S(2)}, u32[]{:S(2)}) collective-permute-start(bf16[4,256,128]{2,1,0:T(8,128)(2,1)S(1)} %get-tuple-element.60), channel_id=1, source_target_pairs={{0,2},{1,3},{2,0},{3,1},{4,6},{5,7},{6,4},{7,5},{8,10},{9,11},{10,... | collective-permute-start | bytes 786440 | tf_op jit(solution)/shard_map/ppermute | solution.py:29
  257.5 3.2 collective-permute-start.30
  260.7 1.4 add_convert_fusion.13
  262.2 2.8 add_convert_fusion.4
  264.9 3.1 collective-permute-start.34
  268.1 3.9 %add_convert_fusion = (bf16[12,128,256]{2,1,0:T(8,128)(2,1)S(1)}, bf16[12,128,256]{2,1,0:T(8,128)(2,1)S(1)}, bf16[12,128,256]{2,1,0:T(8,128)(2,1)S(1)}, bf16[12,128,256]{2,1,0:T(8,128)(2,1)}) fusion(bf16[12,128,256]{2,1,0:T(8,128)(2,1)S(1)} %copy-done.6, bf16[48,128,256]{2,1,0:T(8,128)(2,1)} %collective-permute-done.37, bf16[12,128,256]{2,1,0:T(8,128)(2,1)S(1)} %copy-done.4, ...), kind=kLoop, calls=%fused_computation | loop fusion | flops 6291456 | bytes 9437184 | tf_op jit(solution)/shard_map/convert_element_type | solution.py:53
  272.0 2.0 collective-permute-start.39
  274.0 1.4 add_convert_fusion.8
  275.4 2.2 collective-permute-start.35
  277.6 2.1 collective-permute-start.36
  280.6 40.3 %collective-permute-done.35.refs_2_ = bf16[12,128,128]{2,1,0:T(8,128)(2,1)S(1)} collective-permute-done((bf16[12,128,128]{2,1,0:T(8,128)(2,1)S(1)}, bf16[12,128,128]{2,1,0:T(8,128)(2,1)S(1)}, u32[]{:S(2)}, u32[]{:S(2)}) %collective-permute-start.35) | collective-permute-done | bytes 393248 | tf_op jit(solution)/shard_map/ppermute | solution.py:29
  322.5 4.4 %unpack.1 = (bf16[1024,896]{1,0:T(8,128)(2,1)}, bf16[1024,896]{1,0:T(8,128)(2,1)}, bf16[896,1024]{1,0:T(8,128)(2,1)}) custom-call(s32[64,112]{1,0:T(8,128)} %mask.5, s32[4]{0:T(128)} %pad_add_fusion.where, bf16[12,128,128]{2,1,0:T(8,128)(2,1)} %get-tuple-element.72.refs_0_, ...), custom_call_target="tpu_custom_call", output_to_operand_aliasing={{0}: (10, {}), {1}: (11, {}), {2}: (12, {})} | custom-call | tf_op jit(solution)/shard_map/unpack/pallas_call | solution.py:478
  (139 shorter events, 15.4 us)
Async XLA Ops:
  2.3 18.4 %collective-permute-start = (bf16[4,256,128]{2,1,0:T(8,128)(2,1)}, bf16[4,256,128]{2,1,0:T(8,128)(2,1)}, u32[]{:S(2)}, u32[]{:S(2)}) collective-permute-start(bf16[4,256,128]{2,1,0:T(8,128)(2,1)} %pad_maximum_fusion), channel_id=1, source_target_pairs={{0,4},{1,5},{2,6},{3,7},{4,8},{5,9},{6,10},{7,11},{8,12},{9,13},{1... | collective-permute-start | bytes 786440 | tf_op jit(solution)/shard_map/ppermute | solution.py:29
  3.9 19.0 %collective-permute-start.1 = (bf16[4,256,128]{2,1,0:T(8,128)(2,1)}, bf16[4,256,128]{2,1,0:T(8,128)(2,1)}, u32[]{:S(2)}, u32[]{:S(2)}) collective-permute-start(bf16[4,256,128]{2,1,0:T(8,128)(2,1)} %pad_maximum_fusion), channel_id=1, source_target_pairs={{0,12},{1,13},{2,14},{3,15},{4,0},{5,1},{6,2},{7,3},{8,4},{9,5},{1... | collective-permute-start | bytes 786440 | tf_op jit(solution)/shard_map/ppermute | solution.py:29
  5.6 18.5 %collective-permute-start.2 = (bf16[4,256,128]{2,1,0:T(8,128)(2,1)}, bf16[4,256,128]{2,1,0:T(8,128)(2,1)}, u32[]{:S(2)}, u32[]{:S(2)}) collective-permute-start(bf16[4,256,128]{2,1,0:T(8,128)(2,1)} %pad_maximum_fusion), channel_id=1, source_target_pairs={{0,8},{1,9},{2,10},{3,11},{4,12},{5,13},{6,14},{7,15},{8,0},{9,1},... | collective-permute-start | bytes 786440 | tf_op jit(solution)/shard_map/ppermute | solution.py:29
  12.1 10.9 %copy-start = (bf16[12,128,384]{2,1,0:T(8,128)(2,1)S(1)}, bf16[12,128,384]{2,1,0:T(8,128)(2,1)}, u32[]{:S(2)}) copy-start(bf16[12,128,384]{2,1,0:T(8,128)(2,1)} %pack.1.refs_4_) | copy-start | bytes 3538948
  12.1 29.4 %collective-permute-start.6 = (bf16[12,128,384]{2,1,0:T(8,128)(2,1)}, bf16[12,128,384]{2,1,0:T(8,128)(2,1)S(1)}, u32[]{:S(2)}, u32[]{:S(2)}) collective-permute-start(bf16[12,128,384]{2,1,0:T(8,128)(2,1)} %pack.1.refs_4_), channel_id=1, source_target_pairs={{0,32},{1,33},{2,34},{3,35},{4,36},{5,37},{6,38},{7,39},{8,40},{9,... | collective-permute-start | bytes 3538952 | tf_op jit(solution)/shard_map/ppermute | solution.py:29
  14.1 30.3 %collective-permute-start.7 = (bf16[12,128,384]{2,1,0:T(8,128)(2,1)}, bf16[12,128,384]{2,1,0:T(8,128)(2,1)}, u32[]{:S(2)}, u32[]{:S(2)}) collective-permute-start(bf16[12,128,384]{2,1,0:T(8,128)(2,1)} %pack.1.refs_4_), channel_id=1, source_target_pairs={{0,96},{1,97},{2,98},{3,99},{4,100},{5,101},{6,102},{7,103},{8,104... | collective-permute-start | bytes 3538952 | tf_op jit(solution)/shard_map/ppermute | solution.py:29
  20.7 8.2 %collective-permute-start.21 = (bf16[4,256,128]{2,1,0:T(8,128)(2,1)S(1)}, bf16[4,256,128]{2,1,0:T(8,128)(2,1)S(1)}, u32[]{:S(2)}, u32[]{:S(2)}) collective-permute-start(bf16[4,256,128]{2,1,0:T(8,128)(2,1)S(1)} %pad_maximum_fusion.2), channel_id=1, source_target_pairs={{0,1},{1,2},{2,3},{3,0},{4,5},{5,6},{6,7},{7,4},{8,9},{9,10},{10,1... | collective-permute-start | bytes 786440 | tf_op jit(solution)/shard_map/ppermute | solution.py:29
  23.0 40.8 %collective-permute-start.10 = (bf16[12,128,384]{2,1,0:T(8,128)(2,1)S(1)}, bf16[12,128,384]{2,1,0:T(8,128)(2,1)S(1)}, u32[]{:S(2)}, u32[]{:S(2)}) collective-permute-start(bf16[12,128,384]{2,1,0:T(8,128)(2,1)S(1)} %copy-done), channel_id=1, source_target_pairs={{0,16},{1,17},{2,18},{3,19},{4,20},{5,21},{6,22},{7,23},{8,24},{9,... | collective-permute-start | bytes 3538952 | tf_op jit(solution)/shard_map/ppermute | solution.py:29
  24.1 45.1 %copy-start.26 = (bf16[256,512]{1,0:T(8,128)(2,1)S(1)}, bf16[256,512]{1,0:T(8,128)(2,1)}, u32[]{:S(2)}) copy-start(bf16[256,512]{1,0:T(8,128)(2,1)} %param.7) | copy-start | bytes 786436
  25.1 58.0 %copy-start.15 = (bf16[16,256,128]{2,1,0:T(8,128)(2,1)}, bf16[16,256,128]{2,1,0:T(8,128)(2,1)S(1)}, u32[]{:S(2)}) copy-start(bf16[16,256,128]{2,1,0:T(8,128)(2,1)S(1)} %constant_dynamic-update-slice_fusion.refs_0_) | copy-start | bytes 3145732
  25.1 41.5 %collective-permute-start.3 = (bf16[16,256,128]{2,1,0:T(8,128)(2,1)S(1)}, bf16[16,256,128]{2,1,0:T(8,128)(2,1)S(1)}, u32[]{:S(2)}, u32[]{:S(2)}) collective-permute-start(bf16[16,256,128]{2,1,0:T(8,128)(2,1)S(1)} %constant_dynamic-update-slice_fusion.refs_0_), channel_id=1, source_target_pairs={{0,1},{1,2},{2,3},{3,0},{4,5},{5,6},{6,7},{7,4},{8,9},{9,10},{10,1... | collective-permute-start | bytes 3145736 | tf_op jit(solution)/shard_map/ppermute | solution.py:29
  28.9 15.5 %copy-start.36 = (bf16[4,256,128]{2,1,0:T(8,128)(2,1)}, bf16[4,256,128]{2,1,0:T(8,128)(2,1)S(1)}, u32[]{:S(2)}) copy-start(bf16[4,256,128]{2,1,0:T(8,128)(2,1)S(1)} %collective-permute-done.21) | copy-start | bytes 786436
  28.9 38.8 %collective-permute-start.4 = (bf16[16,256,128]{2,1,0:T(8,128)(2,1)S(1)}, bf16[16,256,128]{2,1,0:T(8,128)(2,1)S(1)}, u32[]{:S(2)}, u32[]{:S(2)}) collective-permute-start(bf16[16,256,128]{2,1,0:T(8,128)(2,1)S(1)} %constant_dynamic-update-slice_fusion.refs_0_), channel_id=1, source_target_pairs={{0,3},{1,0},{2,1},{3,2},{4,7},{5,4},{6,5},{7,6},{8,11},{9,8},{10,9... | collective-permute-start | bytes 3145736 | tf_op jit(solution)/shard_map/ppermute | solution.py:29
  41.5 49.1 %copy-start.13 = (bf16[12,128,384]{2,1,0:T(8,128)(2,1)}, bf16[12,128,384]{2,1,0:T(8,128)(2,1)S(1)}, u32[]{:S(2)}) copy-start(bf16[12,128,384]{2,1,0:T(8,128)(2,1)S(1)} %collective-permute-done.6.refs_5_) | copy-start | bytes 3538948
  41.5 19.0 %collective-permute-start.22 = (bf16[4,256,128]{2,1,0:T(8,128)(2,1)S(1)}, bf16[4,256,128]{2,1,0:T(8,128)(2,1)S(1)}, u32[]{:S(2)}, u32[]{:S(2)}) collective-permute-start(bf16[4,256,128]{2,1,0:T(8,128)(2,1)S(1)} %pad_maximum_fusion.2), channel_id=1, source_target_pairs={{0,3},{1,0},{2,1},{3,2},{4,7},{5,4},{6,5},{7,6},{8,11},{9,8},{10,9... | collective-permute-start | bytes 786440 | tf_op jit(solution)/shard_map/ppermute | solution.py:29
  44.4 16.1 %collective-permute-start.23 = (bf16[4,256,128]{2,1,0:T(8,128)(2,1)S(1)}, bf16[4,256,128]{2,1,0:T(8,128)(2,1)S(1)}, u32[]{:S(2)}, u32[]{:S(2)}) collective-permute-start(bf16[4,256,128]{2,1,0:T(8,128)(2,1)S(1)} %pad_maximum_fusion.2), channel_id=1, source_target_pairs={{0,2},{1,3},{2,0},{3,1},{4,6},{5,7},{6,4},{7,5},{8,10},{9,11},{10,... | collective-permute-start | bytes 786440 | tf_op jit(solution)/shard_map/ppermute | solution.py:29
  60.5 12.8 %copy-start.37 = (bf16[4,256,128]{2,1,0:T(8,128)(2,1)}, bf16[4,256,128]{2,1,0:T(8,128)(2,1)S(1)}, u32[]{:S(2)}) copy-start(bf16[4,256,128]{2,1,0:T(8,128)(2,1)S(1)} %collective-permute-done.22) | copy-start | bytes 786436
  60.5 11.9 %collective-permute-start.8 = (bf16[6,128,384]{2,1,0:T(8,128)(2,1)S(1)}, bf16[6,128,384]{2,1,0:T(8,128)(2,1)}, u32[]{:S(2)}, u32[]{:S(2)}) collective-permute-start(bf16[6,128,384]{2,1,0:T(8,128)(2,1)S(1)} %slice.232), channel_id=1, source_target_pairs={{0,32},{1,33},{2,34},{3,35},{4,36},{5,37},{6,38},{7,39},{8,40},{9,... | collective-permute-start | bytes 1769480 | tf_op jit(solution)/shard_map/ppermute | solution.py:29
  60.6 12.8 %copy-start.38 = (bf16[4,256,128]{2,1,0:T(8,128)(2,1)}, bf16[4,256,128]{2,1,0:T(8,128)(2,1)S(1)}, u32[]{:S(2)}) copy-start(bf16[4,256,128]{2,1,0:T(8,128)(2,1)S(1)} %collective-permute-done.23) | copy-start | bytes 786436
  60.6 12.7 %collective-permute-start.9 = (bf16[6,128,384]{2,1,0:T(8,128)(2,1)S(1)}, bf16[6,128,384]{2,1,0:T(8,128)(2,1)}, u32[]{:S(2)}, u32[]{:S(2)}) collective-permute-start(bf16[6,128,384]{2,1,0:T(8,128)(2,1)S(1)} %slice.233), channel_id=1, source_target_pairs={{0,96},{1,97},{2,98},{3,99},{4,100},{5,101},{6,102},{7,103},{8,104... | collective-permute-start | bytes 1769480 | tf_op jit(solution)/shard_map/ppermute | solution.py:29
  64.8 22.0 %collective-permute-start.5 = (bf16[16,256,128]{2,1,0:T(8,128)(2,1)S(1)}, bf16[16,256,128]{2,1,0:T(8,128)(2,1)}, u32[]{:S(2)}, u32[]{:S(2)}) collective-permute-start(bf16[16,256,128]{2,1,0:T(8,128)(2,1)S(1)} %constant_dynamic-update-slice_fusion.refs_0_), channel_id=1, source_target_pairs={{0,2},{1,3},{2,0},{3,1},{4,6},{5,7},{6,4},{7,5},{8,10},{9,11},{10,... | collective-permute-start | bytes 3145736 | tf_op jit(solution)/shard_map/ppermute | solution.py:29
  67.6 20.2 %collective-permute-start.11 = (bf16[12,128,384]{2,1,0:T(8,128)(2,1)S(1)}, bf16[12,128,384]{2,1,0:T(8,128)(2,1)}, u32[]{:S(2)}, u32[]{:S(2)}) collective-permute-start(bf16[12,128,384]{2,1,0:T(8,128)(2,1)S(1)} %collective-permute-done.6.refs_5_), channel_id=1, source_target_pairs={{0,16},{1,17},{2,18},{3,19},{4,20},{5,21},{6,22},{7,23},{8,24},{9,... | collective-permute-start | bytes 3538952 | tf_op jit(solution)/shard_map/ppermute | solution.py:29
  68.7 21.4 %collective-permute-start.12 = (bf16[12,128,384]{2,1,0:T(8,128)(2,1)}, bf16[12,128,384]{2,1,0:T(8,128)(2,1)}, u32[]{:S(2)}, u32[]{:S(2)}) collective-permute-start(bf16[12,128,384]{2,1,0:T(8,128)(2,1)} %collective-permute-done.7.refs_6_), channel_id=1, source_target_pairs={{0,16},{1,17},{2,18},{3,19},{4,20},{5,21},{6,22},{7,23},{8,24},{9,... | collective-permute-start | bytes 3538952 | tf_op jit(solution)/shard_map/ppermute | solution.py:29
  72.4 18.2 %collective-permute-start.13 = (bf16[6,128,384]{2,1,0:T(8,128)(2,1)}, bf16[6,128,384]{2,1,0:T(8,128)(2,1)}, u32[]{:S(2)}, u32[]{:S(2)}) collective-permute-start(bf16[6,128,384]{2,1,0:T(8,128)(2,1)} %collective-permute-done.8.refs_7_), channel_id=1, source_target_pairs={{0,16},{1,17},{2,18},{3,19},{4,20},{5,21},{6,22},{7,23},{8,24},{9,... | collective-permute-start | bytes 1769480 | tf_op jit(solution)/shard_map/ppermute | solution.py:29
  73.3 17.3 %collective-permute-start.14 = (bf16[6,128,384]{2,1,0:T(8,128)(2,1)}, bf16[6,128,384]{2,1,0:T(8,128)(2,1)}, u32[]{:S(2)}, u32[]{:S(2)}) collective-permute-start(bf16[6,128,384]{2,1,0:T(8,128)(2,1)} %collective-permute-done.9.refs_8_), channel_id=1, source_target_pairs={{0,16},{1,17},{2,18},{3,19},{4,20},{5,21},{6,22},{7,23},{8,24},{9,... | collective-permute-start | bytes 1769480 | tf_op jit(solution)/shard_map/ppermute | solution.py:29
  79.9 10.7 %copy-start.14 = (s32[8,128]{1,0:T(8,128)S(1)}, s32[8,128]{1,0:T(8,128)}, u32[]{:S(2)}) copy-start(s32[8,128]{1,0:T(8,128)} %plan.1.table) | copy-start | bytes 12292
  79.9 10.7 %copy-start.19 = (bf16[12,128,384]{2,1,0:T(8,128)(2,1)S(1)}, bf16[12,128,384]{2,1,0:T(8,128)(2,1)}, u32[]{:S(2)}) copy-start(bf16[12,128,384]{2,1,0:T(8,128)(2,1)} %copy-done.18) | copy-start | bytes 3538948
  86.8 49.1 %collective-permute-start.24 = (bf16[16,256,128]{2,1,0:T(8,128)(2,1)}, bf16[16,256,128]{2,1,0:T(8,128)(2,1)S(1)}, u32[]{:S(2)}, u32[]{:S(2)}) collective-permute-start(bf16[16,256,128]{2,1,0:T(8,128)(2,1)} %constant_dynamic-update-slice_fusion.7.refs_0_), channel_id=1, source_target_pairs={{0,4},{1,5},{2,6},{3,7},{4,8},{5,9},{6,10},{7,11},{8,12},{9,13},{1... | collective-permute-start | bytes 3145736 | tf_op jit(solution)/shard_map/ppermute | solution.py:29
  87.8 48.1 %collective-permute-start.25 = (bf16[16,256,128]{2,1,0:T(8,128)(2,1)}, bf16[16,256,128]{2,1,0:T(8,128)(2,1)S(1)}, u32[]{:S(2)}, u32[]{:S(2)}) collective-permute-start(bf16[16,256,128]{2,1,0:T(8,128)(2,1)} %constant_dynamic-update-slice_fusion.7.refs_0_), channel_id=1, source_target_pairs={{0,12},{1,13},{2,14},{3,15},{4,0},{5,1},{6,2},{7,3},{8,4},{9,5},{1... | collective-permute-start | bytes 3145736 | tf_op jit(solution)/shard_map/ppermute | solution.py:29
  90.1 45.8 %collective-permute-start.26 = (bf16[16,256,128]{2,1,0:T(8,128)(2,1)}, bf16[16,256,128]{2,1,0:T(8,128)(2,1)S(1)}, u32[]{:S(2)}, u32[]{:S(2)}) collective-permute-start(bf16[16,256,128]{2,1,0:T(8,128)(2,1)} %constant_dynamic-update-slice_fusion.7.refs_0_), channel_id=1, source_target_pairs={{0,8},{1,9},{2,10},{3,11},{4,12},{5,13},{6,14},{7,15},{8,0},{9,1},... | collective-permute-start | bytes 3145736 | tf_op jit(solution)/shard_map/ppermute | solution.py:29
  137.6 21.2 %copy-start.17 = (bf16[16,256,128]{2,1,0:T(8,128)(2,1)S(1)}, bf16[16,256,128]{2,1,0:T(8,128)(2,1)}, u32[]{:S(2)}) copy-start(bf16[16,256,128]{2,1,0:T(8,128)(2,1)} %copy-done.15) | copy-start | bytes 3145732
  137.6 21.2 %copy-start.22 = (bf16[16,256,128]{2,1,0:T(8,128)(2,1)S(1)}, bf16[16,256,128]{2,1,0:T(8,128)(2,1)}, u32[]{:S(2)}) copy-start(bf16[16,256,128]{2,1,0:T(8,128)(2,1)} %copy-done.20) | copy-start | bytes 3145732
  137.6 21.3 %copy-start.25 = (bf16[16,256,128]{2,1,0:T(8,128)(2,1)S(1)}, bf16[16,256,128]{2,1,0:T(8,128)(2,1)}, u32[]{:S(2)}) copy-start(bf16[16,256,128]{2,1,0:T(8,128)(2,1)} %copy-done.23) | copy-start | bytes 3145732
  158.8 8.8 %copy-start.7 = (bf16[12,128,128]{2,1,0:T(8,128)(2,1)}, bf16[12,128,128]{2,1,0:T(8,128)(2,1)S(1)}, u32[]{:S(2)}) copy-start(bf16[12,128,128]{2,1,0:T(8,128)(2,1)S(1)} %get-tuple-element.44) | copy-start | bytes 1179652
  158.8 8.8 %copy-start.9 = (bf16[12,128,128]{2,1,0:T(8,128)(2,1)}, bf16[12,128,128]{2,1,0:T(8,128)(2,1)S(1)}, u32[]{:S(2)}) copy-start(bf16[12,128,128]{2,1,0:T(8,128)(2,1)S(1)} %get-tuple-element.45) | copy-start | bytes 1179652
  158.8 8.8 %copy-start.11 = (bf16[12,128,128]{2,1,0:T(8,128)(2,1)}, bf16[12,128,128]{2,1,0:T(8,128)(2,1)S(1)}, u32[]{:S(2)}) copy-start(bf16[12,128,128]{2,1,0:T(8,128)(2,1)S(1)} %get-tuple-element.46) | copy-start | bytes 1179652
  170.3 97.7 %collective-permute-start.37 = (bf16[48,128,256]{2,1,0:T(8,128)(2,1)}, bf16[48,128,256]{2,1,0:T(8,128)(2,1)}, u32[]{:S(2)}, u32[]{:S(2)}) collective-permute-start(bf16[48,128,256]{2,1,0:T(8,128)(2,1)} %get-tuple-element.49), channel_id=1, source_target_pairs={{0,16},{1,17},{2,18},{3,19},{4,20},{5,21},{6,22},{7,23},{8,24},{9,... | collective-permute-start | bytes 9437192 | tf_op jit(solution)/shard_map/ppermute | solution.py:29
  170.3 27.6 %collective-permute-start.17 = (bf16[16,256,128]{2,1,0:T(8,128)(2,1)S(1)}, bf16[16,256,128]{2,1,0:T(8,128)(2,1)S(1)}, u32[]{:S(2)}, u32[]{:S(2)}) collective-permute-start(bf16[16,256,128]{2,1,0:T(8,128)(2,1)S(1)} %get-tuple-element.35), channel_id=1, source_target_pairs={{0,2},{1,3},{2,0},{3,1},{4,6},{5,7},{6,4},{7,5},{8,10},{9,11},{10,... | collective-permute-start | bytes 3145736 | tf_op jit(solution)/shard_map/ppermute | solution.py:29
  171.9 47.9 %collective-permute-start.16 = (bf16[16,256,128]{2,1,0:T(8,128)(2,1)S(1)}, bf16[16,256,128]{2,1,0:T(8,128)(2,1)S(1)}, u32[]{:S(2)}, u32[]{:S(2)}) collective-permute-start(bf16[16,256,128]{2,1,0:T(8,128)(2,1)S(1)} %get-tuple-element.34), channel_id=1, source_target_pairs={{0,1},{1,2},{2,3},{3,0},{4,5},{5,6},{6,7},{7,4},{8,9},{9,10},{10,1... | collective-permute-start | bytes 3145736 | tf_op jit(solution)/shard_map/ppermute | solution.py:29
  176.5 46.1 %collective-permute-start.15 = (bf16[16,256,128]{2,1,0:T(8,128)(2,1)S(1)}, bf16[16,256,128]{2,1,0:T(8,128)(2,1)S(1)}, u32[]{:S(2)}, u32[]{:S(2)}) collective-permute-start(bf16[16,256,128]{2,1,0:T(8,128)(2,1)S(1)} %get-tuple-element.33), channel_id=1, source_target_pairs={{0,3},{1,0},{2,1},{3,2},{4,7},{5,4},{6,5},{7,6},{8,11},{9,8},{10,9... | collective-permute-start | bytes 3145736 | tf_op jit(solution)/shard_map/ppermute | solution.py:29
  176.5 51.6 %collective-permute-start.29 = (bf16[16,256,128]{2,1,0:T(8,128)(2,1)}, bf16[16,256,128]{2,1,0:T(8,128)(2,1)}, u32[]{:S(2)}, u32[]{:S(2)}) collective-permute-start(bf16[16,256,128]{2,1,0:T(8,128)(2,1)} %get-tuple-element.41), channel_id=1, source_target_pairs={{0,8},{1,9},{2,10},{3,11},{4,12},{5,13},{6,14},{7,15},{8,0},{9,1},... | collective-permute-start | bytes 3145736 | tf_op jit(solution)/shard_map/ppermute | solution.py:29
  197.9 24.6 %copy-start.27 = (bf16[16,256,128]{2,1,0:T(8,128)(2,1)}, bf16[16,256,128]{2,1,0:T(8,128)(2,1)S(1)}, u32[]{:S(2)}) copy-start(bf16[16,256,128]{2,1,0:T(8,128)(2,1)S(1)} %collective-permute-done.17) | copy-start | bytes 3145732
  197.9 30.3 %collective-permute-start.28 = (bf16[16,256,128]{2,1,0:T(8,128)(2,1)}, bf16[16,256,128]{2,1,0:T(8,128)(2,1)}, u32[]{:S(2)}, u32[]{:S(2)}) collective-permute-start(bf16[16,256,128]{2,1,0:T(8,128)(2,1)} %get-tuple-element.40), channel_id=1, source_target_pairs={{0,4},{1,5},{2,6},{3,7},{4,8},{5,9},{6,10},{7,11},{8,12},{9,13},{1... | collective-permute-start | bytes 3145736 | tf_op jit(solution)/shard_map/ppermute | solution.py:29
  219.9 26.3 %collective-permute-start.27 = (bf16[16,256,128]{2,1,0:T(8,128)(2,1)}, bf16[16,256,128]{2,1,0:T(8,128)(2,1)}, u32[]{:S(2)}, u32[]{:S(2)}) collective-permute-start(bf16[16,256,128]{2,1,0:T(8,128)(2,1)} %get-tuple-element.39), channel_id=1, source_target_pairs={{0,12},{1,13},{2,14},{3,15},{4,0},{5,1},{6,2},{7,3},{8,4},{9,5},{1... | collective-permute-start | bytes 3145736 | tf_op jit(solution)/shard_map/ppermute | solution.py:29
  223.5 38.6 %collective-permute-start.33 = (bf16[48,128,128]{2,1,0:T(8,128)(2,1)}, bf16[48,128,128]{2,1,0:T(8,128)(2,1)}, u32[]{:S(2)}, u32[]{:S(2)}) collective-permute-start(bf16[48,128,128]{2,1,0:T(8,128)(2,1)} %get-tuple-element.43), channel_id=1, source_target_pairs={{0,16},{1,17},{2,18},{3,19},{4,20},{5,21},{6,22},{7,23},{8,24},{9,... | collective-permute-start | bytes 4718600 | tf_op jit(solution)/shard_map/ppermute | solution.py:29
  228.1 20.9 %collective-permute-start.20 = (bf16[4,256,128]{2,1,0:T(8,128)(2,1)S(1)}, bf16[4,256,128]{2,1,0:T(8,128)(2,1)S(1)}, u32[]{:S(2)}, u32[]{:S(2)}) collective-permute-start(bf16[4,256,128]{2,1,0:T(8,128)(2,1)S(1)} %get-tuple-element.63), channel_id=1, source_target_pairs={{0,8},{1,9},{2,10},{3,11},{4,12},{5,13},{6,14},{7,15},{8,0},{9,1},... | collective-permute-start | bytes 786440 | tf_op jit(solution)/shard_map/ppermute | solution.py:29
  228.2 29.3 %collective-permute-start.19 = (bf16[4,256,128]{2,1,0:T(8,128)(2,1)S(1)}, bf16[4,256,128]{2,1,0:T(8,128)(2,1)S(1)}, u32[]{:S(2)}, u32[]{:S(2)}) collective-permute-start(bf16[4,256,128]{2,1,0:T(8,128)(2,1)S(1)} %get-tuple-element.64), channel_id=1, source_target_pairs={{0,4},{1,5},{2,6},{3,7},{4,8},{5,9},{6,10},{7,11},{8,12},{9,13},{1... | collective-permute-start | bytes 786440 | tf_op jit(solution)/shard_map/ppermute | solution.py:29
  246.2 11.3 %collective-permute-start.18 = (bf16[4,256,128]{2,1,0:T(8,128)(2,1)S(1)}, bf16[4,256,128]{2,1,0:T(8,128)(2,1)S(1)}, u32[]{:S(2)}, u32[]{:S(2)}) collective-permute-start(bf16[4,256,128]{2,1,0:T(8,128)(2,1)S(1)} %get-tuple-element.62), channel_id=1, source_target_pairs={{0,12},{1,13},{2,14},{3,15},{4,0},{5,1},{6,2},{7,3},{8,4},{9,5},{1... | collective-permute-start | bytes 786440 | tf_op jit(solution)/shard_map/ppermute | solution.py:29
  249.0 13.1 %copy-start.8 = (bf16[12,128,128]{2,1,0:T(8,128)(2,1)S(1)}, bf16[12,128,128]{2,1,0:T(8,128)(2,1)}, u32[]{:S(2)}) copy-start(bf16[12,128,128]{2,1,0:T(8,128)(2,1)} %copy-done.7) | copy-start | bytes 1179652
  249.0 13.1 %copy-start.10 = (bf16[12,128,128]{2,1,0:T(8,128)(2,1)S(1)}, bf16[12,128,128]{2,1,0:T(8,128)(2,1)}, u32[]{:S(2)}) copy-start(bf16[12,128,128]{2,1,0:T(8,128)(2,1)} %copy-done.9) | copy-start | bytes 1179652
  249.0 13.1 %copy-start.12 = (bf16[12,128,128]{2,1,0:T(8,128)(2,1)S(1)}, bf16[12,128,128]{2,1,0:T(8,128)(2,1)}, u32[]{:S(2)}) copy-start(bf16[12,128,128]{2,1,0:T(8,128)(2,1)} %copy-done.11) | copy-start | bytes 1179652
  249.0 23.0 %collective-permute-start.32 = (bf16[4,256,128]{2,1,0:T(8,128)(2,1)S(1)}, bf16[4,256,128]{2,1,0:T(8,128)(2,1)S(1)}, u32[]{:S(2)}, u32[]{:S(2)}) collective-permute-start(bf16[4,256,128]{2,1,0:T(8,128)(2,1)S(1)} %get-tuple-element.60), channel_id=1, source_target_pairs={{0,2},{1,3},{2,0},{3,1},{4,6},{5,7},{6,4},{7,5},{8,10},{9,11},{10,... | collective-permute-start | bytes 786440 | tf_op jit(solution)/shard_map/ppermute | solution.py:29
  257.5 16.5 %collective-permute-start.31 = (bf16[4,256,128]{2,1,0:T(8,128)(2,1)S(1)}, bf16[4,256,128]{2,1,0:T(8,128)(2,1)S(1)}, u32[]{:S(2)}, u32[]{:S(2)}) collective-permute-start(bf16[4,256,128]{2,1,0:T(8,128)(2,1)S(1)} %get-tuple-element.61), channel_id=1, source_target_pairs={{0,1},{1,2},{2,3},{3,0},{4,5},{5,6},{6,7},{7,4},{8,9},{9,10},{10,1... | collective-permute-start | bytes 786440 | tf_op jit(solution)/shard_map/ppermute | solution.py:29
  257.5 16.5 %collective-permute-start.30 = (bf16[4,256,128]{2,1,0:T(8,128)(2,1)S(1)}, bf16[4,256,128]{2,1,0:T(8,128)(2,1)S(1)}, u32[]{:S(2)}, u32[]{:S(2)}) collective-permute-start(bf16[4,256,128]{2,1,0:T(8,128)(2,1)S(1)} %get-tuple-element.59), channel_id=1, source_target_pairs={{0,3},{1,0},{2,1},{3,2},{4,7},{5,4},{6,5},{7,6},{8,11},{9,8},{10,9... | collective-permute-start | bytes 786440 | tf_op jit(solution)/shard_map/ppermute | solution.py:29
  262.1 5.9 %copy-start.2 = (bf16[12,128,256]{2,1,0:T(8,128)(2,1)S(1)}, bf16[12,128,256]{2,1,0:T(8,128)(2,1)}, u32[]{:S(2)}) copy-start(bf16[12,128,256]{2,1,0:T(8,128)(2,1)} %copy-done.1) | copy-start | bytes 2359300
  262.1 5.9 %copy-start.4 = (bf16[12,128,256]{2,1,0:T(8,128)(2,1)S(1)}, bf16[12,128,256]{2,1,0:T(8,128)(2,1)}, u32[]{:S(2)}) copy-start(bf16[12,128,256]{2,1,0:T(8,128)(2,1)} %copy-done.3) | copy-start | bytes 2359300
  262.2 5.9 %copy-start.6 = (bf16[12,128,256]{2,1,0:T(8,128)(2,1)S(1)}, bf16[12,128,256]{2,1,0:T(8,128)(2,1)}, u32[]{:S(2)}) copy-start(bf16[12,128,256]{2,1,0:T(8,128)(2,1)} %copy-done.5) | copy-start | bytes 2359300
  264.9 12.6 %collective-permute-start.34 = (bf16[12,128,128]{2,1,0:T(8,128)(2,1)S(1)}, bf16[12,128,128]{2,1,0:T(8,128)(2,1)S(1)}, u32[]{:S(2)}, u32[]{:S(2)}) collective-permute-start(bf16[12,128,128]{2,1,0:T(8,128)(2,1)S(1)} %get-tuple-element.71), channel_id=1, source_target_pairs={{0,96},{1,97},{2,98},{3,99},{4,100},{5,101},{6,102},{7,103},{8,104... | collective-permute-start | bytes 1179656 | tf_op jit(solution)/shard_map/ppermute | solution.py:29
  272.0 48.9 %collective-permute-start.38 = (bf16[12,128,256]{2,1,0:T(8,128)(2,1)S(1)}, bf16[12,128,256]{2,1,0:T(8,128)(2,1)S(1)}, u32[]{:S(2)}, u32[]{:S(2)}) collective-permute-start(bf16[12,128,256]{2,1,0:T(8,128)(2,1)S(1)} %get-tuple-element.67), channel_id=1, source_target_pairs={{0,96},{1,97},{2,98},{3,99},{4,100},{5,101},{6,102},{7,103},{8,104... | collective-permute-start | bytes 2359304 | tf_op jit(solution)/shard_map/ppermute | solution.py:29
  272.0 48.9 %collective-permute-start.39 = (bf16[12,128,256]{2,1,0:T(8,128)(2,1)S(1)}, bf16[12,128,256]{2,1,0:T(8,128)(2,1)S(1)}, u32[]{:S(2)}, u32[]{:S(2)}) collective-permute-start(bf16[12,128,256]{2,1,0:T(8,128)(2,1)S(1)} %get-tuple-element.66), channel_id=1, source_target_pairs={{0,32},{1,33},{2,34},{3,35},{4,36},{5,37},{6,38},{7,39},{8,40},{9,... | collective-permute-start | bytes 2359304 | tf_op jit(solution)/shard_map/ppermute | solution.py:29
  274.0 46.9 %collective-permute-start.40 = (bf16[12,128,256]{2,1,0:T(8,128)(2,1)S(1)}, bf16[12,128,256]{2,1,0:T(8,128)(2,1)S(1)}, u32[]{:S(2)}, u32[]{:S(2)}) collective-permute-start(bf16[12,128,256]{2,1,0:T(8,128)(2,1)S(1)} %get-tuple-element.65), channel_id=1, source_target_pairs={{0,64},{1,65},{2,66},{3,67},{4,68},{5,69},{6,70},{7,71},{8,72},{9,... | collective-permute-start | bytes 2359304 | tf_op jit(solution)/shard_map/ppermute | solution.py:29
  275.4 45.5 %collective-permute-start.35 = (bf16[12,128,128]{2,1,0:T(8,128)(2,1)S(1)}, bf16[12,128,128]{2,1,0:T(8,128)(2,1)S(1)}, u32[]{:S(2)}, u32[]{:S(2)}) collective-permute-start(bf16[12,128,128]{2,1,0:T(8,128)(2,1)S(1)} %get-tuple-element.70), channel_id=1, source_target_pairs={{0,32},{1,33},{2,34},{3,35},{4,36},{5,37},{6,38},{7,39},{8,40},{9,... | collective-permute-start | bytes 1179656 | tf_op jit(solution)/shard_map/ppermute | solution.py:29
  277.6 43.4 %copy-start.33 = (bf16[12,128,128]{2,1,0:T(8,128)(2,1)}, bf16[12,128,128]{2,1,0:T(8,128)(2,1)S(1)}, u32[]{:S(2)}) copy-start(bf16[12,128,128]{2,1,0:T(8,128)(2,1)S(1)} %collective-permute-done.34.refs_1_) | copy-start | bytes 1179652
  277.6 43.3 %collective-permute-start.36 = (bf16[12,128,128]{2,1,0:T(8,128)(2,1)S(1)}, bf16[12,128,128]{2,1,0:T(8,128)(2,1)S(1)}, u32[]{:S(2)}, u32[]{:S(2)}) collective-permute-start(bf16[12,128,128]{2,1,0:T(8,128)(2,1)S(1)} %get-tuple-element.69), channel_id=1, source_target_pairs={{0,64},{1,65},{2,66},{3,67},{4,68},{5,69},{6,70},{7,71},{8,72},{9,... | collective-permute-start | bytes 1179656 | tf_op jit(solution)/shard_map/ppermute | solution.py:29
  (19 other events, 22.7 us)
where the time goes:
time: 329 us; the launch traced here: 327 us
  waiting for transfers between devices  160 us (49%)
  Pallas kernels  62.5 us (19%)
  starting transfers between devices  56.2 us (17%)
  local copies, waits for them, and re-layouts  31.6 us (10%)
  other arithmetic  15.7 us (5%)
    ppermute x41, waiting for transfers between devices, send(): return lax.ppermute(v, ('row', 'col'), shift(axis, k))  160 us
    ppermute x41, starting transfers between devices, send(): return lax.ppermute(v, ('row', 'col'), shift(axis, k))  56.2 us
    unnamed x96, local copies, waits for them, and re-layouts  25.8 us
    pallas_call x1, Pallas kernels, input_work(): pl.pallas_call(input_body, out_shape=part_shapes(256, BLK) + grad_shapes(...  21.2 us
    pallas_call x1, Pallas kernels, forward_work(): pl.pallas_call(forward_body, out_shape=part_shapes(256, BLK) + [jax.Shape...  15.8 us
    convert_element_type x6, other arithmetic, add(): return total.astype(BF)  13.4 us
    pallas_call x1, Pallas kernels, grad_work(): pl.pallas_call(grad_body, out_shape=grad_shapes(2 * BLK), in_specs=[SMEM,...  8.75 us
  transfers between devices with their start and end apart: 41, of which 12 were waited for; matrix products, arithmetic and copies ran while one was open for 10% of the time, Pallas kernels for 9%

commit v1 on v0

--- a/solution.py
+++ b/solution.py
@@ -55,6 +55,10 @@
 
 def place(d):
     return jnp.where(d == 0, 0, jnp.where(d == 1, 2, jnp.where(d == 2, 3, 1)))
+
+
+def place_back(p):
+    return jnp.where(p == 0, 0, jnp.where(p == 1, 3, jnp.where(p == 2, 1, 2)))
 
 
 def pack_body(mask, where, gate, up, down, out, sems):
@@ -72,19 +76,19 @@
             ),
         )
 
-    def tile_row(i, n):
-        for j in range(7):
+    def tile_col(j, n):
+        for i in range(8):
             m = mask[row * 8 + i, col * 7 + j]
 
             @pl.when((m != 0) & (n < CAP))
-            def _(n=n, j=j):
+            def _(n=n, i=i):
                 for copy in copies(n, i, j):
                     copy.start()
 
             n = n + m
         return n
 
-    n = lax.fori_loop(0, 8, tile_row, jnp.int32(0))
+    n = lax.fori_loop(0, 7, tile_col, jnp.int32(0))
 
     def finish(s, _):
         for copy in copies(s, 0, 0):
@@ -110,35 +114,47 @@
 def plan_body(mask, where, table):
     z, core, x, y = where[0], where[1], where[2], where[3]
     col = x * 4 + y
-    total = jnp.int32(0)
-    for q in range(8):
-        group = ((z + DIST[q % 4]) & 3) * 2 + (core ^ (q // 4))
-
-        def tile_row(i, carry, q=q, group=group):
-            total, slot = carry
-            owner = group * 2 + i // 4
-            sub = i % 4
-            px = place((owner // 4 - x) & 3)
-            py = place((owner % 4 - y) & 3)
-            at_x_y = (py * 4 + px) * 4 + sub
-            at_y_x = (px * 4 + py) * 4 + sub
-            for j in range(7):
-                m = mask[group * 8 + i, col * 7 + j]
-                table[0, total] = slot
-                table[1, total] = at_x_y
-                table[2, total] = at_y_x
+
+    def spot(k, _):
+        q = k // 8
+        d = place_back(q % 4)
+        owner = (((z + d) & 3) * 2 + (core ^ (q // 4))) * 2 + (k % 8) // 4
+        px = place((owner // 4 - x) & 3)
+        py = place((owner % 4 - y) & 3)
+        table[5, k] = (py * 4 + px) * 4 + k % 4
+        table[6, k] = (px * 4 + py) * 4 + k % 4
+        return 0
+
+    lax.fori_loop(0, 64, spot, 0)
+    groups = [((z + DIST[q % 4]) & 3) * 2 + (core ^ (q // 4)) for q in range(8)]
+
+    def tile_col(j, carry):
+        total, slots = carry[0], list(carry[1:])
+        for q in range(8):
+            for i in range(8):
+                m = mask[groups[q] * 8 + i, col * 7 + j]
+                table[0, total] = slots[q]
+                table[1, total] = table[5, q * 8 + i]
+                table[2, total] = table[6, q * 8 + i]
                 table[3, total] = j
-                slot = slot + m
+                slots[q] = slots[q] + m
                 total = total + m
-            return total, slot
-
-        total, _ = lax.fori_loop(0, 8, tile_row, (total, jnp.int32(q * CAP)))
+        for k in range(UNROLL):
+            table[0, total + k] = 8 * CAP
+            table[1, total + k] = 0
+            table[2, total + k] = 0
+            table[3, total + k] = j
+        total = ((total + (UNROLL - 1)) // UNROLL) * UNROLL
+        return (total, *slots)
+
+    start = (jnp.int32(0), *(jnp.int32(q * CAP) for q in range(8)))
+    total = lax.fori_loop(0, 7, tile_col, start)[0]
     for k in range(UNROLL):
         table[0, total + k] = 8 * CAP
         table[1, total + k] = 0
         table[2, total + k] = 0
         table[3, total + k] = 0
-    table[4, 0] = (total + (UNROLL - 1)) // UNROLL
+    table[4, 0] = (total // UNROLL + 1) // 2
 
 
 def plan(mask, where):
@@ -152,6 +168,9 @@
     )(mask, where)
 
 
+SMEM = pl.BlockSpec(memory_space=pltpu.SMEM)
+HBM = pl.BlockSpec(memory_space=pl.ANY)
+IN_VMEM = pl.BlockSpec(memory_space=pltpu.VMEM)
 NT = (((1,), (1,)), ((), ()))
 TN = (((0,), (0,)), ((), ()))
 
@@ -193,40 +212,82 @@
     lax.fori_loop(0, ref.shape[0], body, 0)
 
 
-def settle(rows, sums):
-    def body(p, _):
-        sums[p] = rows[p].astype(BF)
-        return 0
-
-    lax.fori_loop(0, 64, body, 0)
+def settle(rows, sums, parts, sems, first):
+    copies = []
+    for k, part in enumerate(parts):
+        def body(p, _):
+            for r in range(4):
+                sums[p * 4 + r] = rows[p * 4 + r].astype(BF)
+            return 0
+
+        lax.fori_loop(k * 4, k * 4 + 4, body, 0)
+        copies.append(pltpu.make_async_copy(sums.at[pl.ds(k * 16, 16)], part, sems.at[first + k]))
+        copies[-1].start()
+    return copies
+
+
+def step(table, i, spots):
+    at = i * UNROLL
+    return (
+        [table[0, at + k] for k in range(UNROLL)],
+        [table[spots, at + k] for k in range(UNROLL)],
+        table[3, at],
+    )
+
+
+def side(values, axis):
+    return [jnp.concatenate(values[k : k + 2], axis) for k in range(0, UNROLL, 2)]
+
+
+GU = slice(0, 2 * BLK)
+DOWN = slice(2 * BLK, 3 * BLK)
+
+
+def stage_body(*refs):
+    parts, out, sems = refs[:10], refs[10], refs[11]
+    copies = fetch(parts, out, sems, 0)
+    out[8 * CAP] = jnp.zeros((BLK, 3 * BLK), BF)
+    wait(copies)
+
+
+def stage(parts):
+    return pl.pallas_call(
+        stage_body,
+        out_shape=jax.ShapeDtypeStruct((8 * CAP + 1, BLK, 3 * BLK), BF),
+        in_specs=[HBM] * 10,
+        out_specs=IN_VMEM,
+        scratch_shapes=[pltpu.SemaphoreType.DMA((10,))],
+        name="stage",
+    )(*parts)
+
+
+def in_pairs(steps, body):
+    def turn(i, _):
+        body(i * 2)
+        body(i * 2 + 1)
+        return 0
+
+    lax.fori_loop(0, steps, turn, 0)
 
 
 def forward_body(table, *refs):
     token_parts, refs = refs[:4], refs[4:]
-    weight_parts, refs = refs[:10], refs[10:]
+    weights, refs = refs[0], refs[1:]
     outs, refs = refs[:4], refs[4:]
-    gu, hidden, acts, weights, rows, sums, sems = refs
-    loads = fetch(token_parts, acts, sems, 0) + fetch(weight_parts, weights, sems, 4)
-    weights[8 * CAP] = jnp.zeros((BLK, 3 * BLK), BF)
+    gu, hidden, acts, rows, sums, sems = refs
+    loads = fetch(token_parts, acts, sems, 0)
     clear(gu)
     clear(rows)
     wait(loads)
     steps = table[4, 0]
 
-    def entry(k):
-        return table[0, k], table[1, k], table[3, k]
-
-    def forward(i, _):
-        es = [entry(i * UNROLL + k) for k in range(UNROLL)]
-        ds = [
-            jnp.dot(acts[t], weights[s, :, : 2 * BLK], preferred_element_type=F32)
-            for s, t, _ in es
-        ]
-        for (_, _, c), d in zip(es, ds):
-            gu[c] += d
-        return 0
-
-    lax.fori_loop(0, steps, forward, 0)
+    def forward(i):
+        slots, spots, c = step(table, i, 1)
+        lhs = side([acts[t] for t in spots], 1)
+        rhs = side([weights[s, :, GU] for s in slots], 0)
+        gu[c] += sum(jnp.dot(a, b, preferred_element_type=F32) for a, b in zip(lhs, rhs))
+
+    in_pairs(steps, forward)
 
     def activate(c, _):
         g = gu[c, :, :BLK]
@@ -235,24 +296,16 @@
 
     lax.fori_loop(0, 7, activate, 0)
 
-    def output(i, _):
-        es = [entry(i * UNROLL + k) for k in range(UNROLL)]
-        ds = [
-            jnp.dot(hidden[c], weights[s, :, 2 * BLK :], preferred_element_type=F32)
-            for s, _, c in es
-        ]
-        for (_, t, _), d in zip(es, ds):
-            rows[t] += d
-        return 0
-
-    lax.fori_loop(0, steps, output, 0)
-    settle(rows, sums)
-    wait(store(outs, sums, sems, 0))
-
-
-SMEM = pl.BlockSpec(memory_space=pltpu.SMEM)
-HBM = pl.BlockSpec(memory_space=pl.ANY)
-IN_VMEM = pl.BlockSpec(memory_space=pltpu.VMEM)
+    def output(i):
+        slots, spots, c = step(table, i, 1)
+        h = hidden[c]
+        rhs = side([weights[s, :, DOWN] for s in slots], 1)
+        ds = [jnp.dot(h, b, preferred_element_type=F32) for b in rhs]
+        for k, t in enumerate(spots):
+            rows[t] += ds[k // 2][:, (k % 2) * BLK : (k % 2) * BLK + BLK]
+
+    in_pairs(steps, output)
+    wait(settle(rows, sums, outs, sems, 0))
 
 
 def cost(tiles, moved):
@@ -265,60 +318,50 @@
     return [jax.ShapeDtypeStruct((16, *tail), BF)] * 4
 
 
-def forward_work(table, token_parts, weight_parts):
+def forward_work(table, token_parts, weights):
     vmem = pltpu.VMEM
     return pl.pallas_call(
         forward_body,
         out_shape=part_shapes(256, BLK)
         + [jax.ShapeDtypeStruct((7, 256, 2 * BLK), F32), jax.ShapeDtypeStruct((7, 256, BLK), BF)],
-        in_specs=[SMEM] + [HBM] * 14,
+        in_specs=[SMEM] + [HBM] * 4 + [IN_VMEM],
         out_specs=[HBM] * 4 + [IN_VMEM] * 2,
         scratch_shapes=[
             vmem((64, 256, BLK), BF),
-            vmem((8 * CAP + 1, BLK, 3 * BLK), BF),
             vmem((64, 256, BLK), F32),
             vmem((64, 256, BLK), BF),
             pltpu.SemaphoreType.DMA((14,)),
         ],
-        compiler_params=pltpu.CompilerParams(vmem_limit_bytes=36 * MIB),
+        compiler_params=pltpu.CompilerParams(vmem_limit_bytes=20 * MIB),
         cost_estimate=cost(56 * 3 * 4, 20 * MIB),
         name="forward",
-    )(table, *token_parts, *weight_parts)
+    )(table, *token_parts, weights)
 
 
 def input_body(table, gu, hidden, *refs):
     cot_parts, refs = refs[:4], refs[4:]
-    weight_parts, refs = refs[:10], refs[10:]
+    weights, refs = refs[0], refs[1:]
     outs, refs = refs[:4], refs[4:]
     grads, refs = refs[:5], refs[5:]
-    gucot, cots, weights, hgrad, rows, sums, gsum, sems = refs
-    loads = fetch(cot_parts, cots, sems, 0) + fetch(weight_parts, weights, sems, 4)
-    weights[8 * CAP] = jnp.zeros((BLK, 3 * BLK), BF)
+    gucot, cots, hgrad, rows, sums, gsum, sems = refs
+    loads = fetch(cot_parts, cots, sems, 0)
     clear(hgrad)
     clear(rows)
     wait(loads)
     steps = table[4, 0]
 
-    def entry(k):
-        return table[0, k], table[2, k], table[3, k]
-
-    def middle(i, _):
-        es = [entry(i * UNROLL + k) for k in range(UNROLL)]
-        res = []
-        for s, t, c in es:
-            g = cots[t]
-            res.append(
-                (
-                    lax.dot_general(g, weights[s, :, 2 * BLK :], NT, preferred_element_type=F32),
-                    lax.dot_general(hidden[c], g, TN, preferred_element_type=F32),
-                )
-            )
-        for (s, _, c), (hg, dg) in zip(es, res):
-            hgrad[c] += hg
-            gsum[s] = dg.astype(BF)
-        return 0
-
-    lax.fori_loop(0, steps, middle, 0)
+    def middle(i):
+        slots, spots, c = step(table, i, 2)
+        gs = [cots[t] for t in spots]
+        lhs = side(gs, 1)
+        rhs = side([weights[s, :, DOWN] for s in slots], 1)
+        hg = sum(lax.dot_general(a, b, NT, preferred_element_type=F32) for a, b in zip(lhs, rhs))
+        ds = [lax.dot_general(hidden[c], a, TN, preferred_element_type=F32) for a in lhs]
+        hgrad[c] += hg
+        for k, s in enumerate(slots):
+            gsum[s] = ds[k // 2][:, (k % 2) * BLK : (k % 2) * BLK + BLK].astype(BF)
+
+    in_pairs(steps, middle)
     stores = store(grads, gsum, sems, 0)
 
     def cotangents(c, _):
@@ -331,47 +374,43 @@
 
     lax.fori_loop(0, 7, cotangents, 0)
 
-    def backward(i, _):
-        es = [entry(i * UNROLL + k) for k in range(UNROLL)]
-        res = [
-            lax.dot_general(gucot[c], weights[s, :, : 2 * BLK], NT, preferred_element_type=F32)
-            for s, _, c in es
-        ]
-        for (_, t, _), r in zip(es, res):
-            rows[t] += r
-        return 0
-
-    lax.fori_loop(0, steps, backward, 0)
-    settle(rows, sums)
-    wait(stores + store(outs, sums, sems, 5))
+    def backward(i):
+        slots, spots, c = step(table, i, 2)
+        d = gucot[c]
+        rhs = side([weights[s, :, GU] for s in slots], 0)
+        ds = [lax.dot_general(d, b, NT, preferred_element_type=F32) for b in rhs]
+        for k, t in enumerate(spots):
+            rows[t] += ds[k // 2][:, (k % 2) * BLK : (k % 2) * BLK + BLK]
+
+    in_pairs(steps, backward)
+    wait(stores + settle(rows, sums, outs, sems, 5))
 
 
 def grad_shapes(width):
     return [jax.ShapeDtypeStruct((n, BLK, width), BF) for n in (12, 12, 12, 12, 48)]
 
 
-def input_work(table, gu, hidden, cot_parts, weight_parts):
+def input_work(table, gu, hidden, cot_parts, weights):
     vmem = pltpu.VMEM
     return pl.pallas_call(
         input_body,
         out_shape=part_shapes(256, BLK)
         + grad_shapes(BLK)
         + [jax.ShapeDtypeStruct((7, 256, 2 * BLK), BF)],
-        in_specs=[SMEM] + [IN_VMEM] * 2 + [HBM] * 14,
+        in_specs=[SMEM] + [IN_VMEM] * 2 + [HBM] * 4 + [IN_VMEM],
         out_specs=[HBM] * 9 + [IN_VMEM],
         scratch_shapes=[
             vmem((64, 256, BLK), BF),
-            vmem((8 * CAP + 1, BLK, 3 * BLK), BF),
             vmem((7, 256, BLK), F32),
             vmem((64, 256, BLK), F32),
             vmem((64, 256, BLK), BF),
             vmem((8 * CAP + 1, BLK, BLK), BF),
             pltpu.SemaphoreType.DMA((14,)),
         ],
-        compiler_params=pltpu.CompilerParams(vmem_limit_bytes=44 * MIB),
+        compiler_params=pltpu.CompilerParams(vmem_limit_bytes=24 * MIB),
         cost_estimate=cost(56 * 4 * 4, 22 * MIB),
         name="inputs",
-    )(table, gu, hidden, *cot_parts, *weight_parts)
+    )(table, gu, hidden, *cot_parts, weights)
 
 
 def grad_body(table, gucot, *refs):
@@ -381,19 +420,15 @@
     wait(fetch(token_parts, acts, sems, 0))
     steps = table[4, 0]
 
-    def backward(i, _):
-        es = [
-            (table[0, i * UNROLL + k], table[1, i * UNROLL + k], table[3, i * UNROLL + k])
-            for k in range(UNROLL)
-        ]
-        res = [
-            lax.dot_general(acts[t], gucot[c], TN, preferred_element_type=F32) for _, t, c in es
-        ]
-        for (s, _, _), r in zip(es, res):
-            gsum[s] = r.astype(BF)
-        return 0
-
-    lax.fori_loop(0, steps, backward, 0)
+    def backward(i):
+        slots, spots, c = step(table, i, 1)
+        lhs = side([acts[t] for t in spots], 1)
+        d = gucot[c]
+        res = [lax.dot_general(a, d, TN, preferred_element_type=F32) for a in lhs]
+        for k, s in enumerate(slots):
+            gsum[s] = res[k // 2][(k % 2) * BLK : (k % 2) * BLK + BLK].astype(BF)
+
+    in_pairs(steps, backward)
     wait(store(grads, gsum, sems, 0))
 
 
@@ -409,7 +444,7 @@
             vmem((8 * CAP + 1, BLK, 2 * BLK), BF),
             pltpu.SemaphoreType.DMA((5,)),
         ],
-        compiler_params=pltpu.CompilerParams(vmem_limit_bytes=20 * MIB),
+        compiler_params=pltpu.CompilerParams(vmem_limit_bytes=14 * MIB),
         cost_estimate=cost(56 * 2 * 4, 10 * MIB),
         name="grads",
     )(table, gucot, *token_parts)
@@ -452,19 +487,19 @@
             ),
         )
 
-    def tile_row(i, n):
-        for j in range(7):
+    def tile_col(j, n):
+        for i in range(8):
             m = mask[row * 8 + i, col * 7 + j]
 
             @pl.when((m != 0) & (n < CAP))
-            def _(n=n, j=j):
+            def _(n=n, i=i):
                 for copy in copies(n, i, j):
                     copy.start()
 
             n = n + m
         return n
 
-    n = lax.fori_loop(0, 8, tile_row, jnp.int32(0))
+    n = lax.fori_loop(0, 7, tile_col, jnp.int32(0))
 
     def finish(s, _):
         for copy in copies(s, 0, 0):
@@ -515,11 +550,12 @@
     a, b, c, d = ring_gather(packed, "z")
     mine = [packed, a, b, c, d]
     weight_parts = mine + [send(v, "core", 1) for v in mine]
+    weights = stage(weight_parts)
     cot_parts = gather(cotangent, "y", "x")
 
-    *outs, gu, hidden = forward_work(table, token_parts, weight_parts)
+    *outs, gu, hidden = forward_work(table, token_parts, weights)
     outs = scatter_four(outs, "y")
-    res = input_work(table, gu, hidden, cot_parts, weight_parts)
+    res = input_work(table, gu, hidden, cot_parts, weights)
     ins, downs, gucot = res[:4], res[4:9], res[9]
     ins = scatter_four(ins, "x")
     downs = scatter_four(row_sums(downs), "z")

time: 329 us -> 303 us (0.921)
  local copies, waits for them, and re-layouts: 31.6 us -> 14.6 us
  starting transfers between devices: 56.2 us -> 49.2 us
  Pallas kernels: 62.5 us -> 57.9 us
    unnamed x96 -> x88, local copies, waits for them, and re-layouts: 25.8 us -> 13.3 us
    pallas_call x1, Pallas kernels: 21.2 us -> 13.4 us  [input_work(): pl.pallas_call(input_body, out_shape=part_shapes(256, BLK) + grad_shapes(...]
    pallas_call x0 -> x1, Pallas kernels: none -> 7.48 us  [stage(): pl.pallas_call(stage_body, out_shape=jax.ShapeDtypeStruct((8 * CAP + 1, B...]
    ppermute x41, starting transfers between devices: 56.2 us -> 49.2 us  [send(): return lax.ppermute(v, ('row', 'col'), shift(axis, k))]
    pallas_call x1, Pallas kernels: 15.8 us -> 10.3 us  [forward_work(): pl.pallas_call(forward_body, out_shape=part_shapes(256, BLK) + [jax.Shape...]
    ppermute x41, waiting for transfers between devices: 160 us -> 163 us  [send(): return lax.ppermute(v, ('row', 'col'), shift(axis, k))]
  transfers between devices with their start and end apart: 41 -> 41, of which waited for: 12 -> 13; matrix products, arithmetic and copies ran while one was open for 10% -> 6% of each run, Pallas kernels for 9% -> 9%
where the time goes in v1:
time: 303 us; the launch traced here: 301 us
  waiting for transfers between devices  163 us (54%)
  Pallas kernels  57.9 us (19%)
  starting transfers between devices  49.2 us (16%)
  other arithmetic  15 us (5%)
  local copies, waits for them, and re-layouts  14.6 us (5%)
    ppermute x41, waiting for transfers between devices, send(): return lax.ppermute(v, ('row', 'col'), shift(axis, k))  163 us
    ppermute x41, starting transfers between devices, send(): return lax.ppermute(v, ('row', 'col'), shift(axis, k))  49.2 us
    pallas_call x1, Pallas kernels, input_work(): pl.pallas_call(input_body, out_shape=part_shapes(256, BLK) + grad_shapes(...  13.4 us
    convert_element_type x6, other arithmetic, add(): return total.astype(BF)  13.3 us
    unnamed x88, local copies, waits for them, and re-layouts  13.3 us
    pallas_call x1, Pallas kernels, forward_work(): pl.pallas_call(forward_body, out_shape=part_shapes(256, BLK) + [jax.Shape...  10.3 us
    pallas_call x1, Pallas kernels, plan(): pl.pallas_call(plan_body, out_shape=jax.ShapeDtypeStruct((8, 128), jnp.in...  7.94 us
    pallas_call x1, Pallas kernels, grad_work(): pl.pallas_call(grad_body, out_shape=grad_shapes(2 * BLK), in_specs=[SMEM,...  7.7 us
  transfers between devices with their start and end apart: 41, of which 13 were waited for; matrix products, arithmetic and copies ran while one was open for 6% of the time, Pallas kernels for 9%

profile of v1, /device:TPU:0, one launch (start us, length us, event | category | flops | bytes accessed | tf_op | source)
XLA Modules:
  0.0 301.3 jit_solution(17905445325047543216)
XLA Ops:
  1.3 4.1 %pack.1.refs_0_ = bf16[12,128,384]{2,1,0:T(8,128)(2,1)} custom-call(s32[64,112]{1,0:T(8,128)} %mask.5, s32[4]{0:T(128)} %pad_add_fusion.where, bf16[1024,896]{1,0:T(8,128)(2,1)} %gate.1, bf16[1024,896]{1,0:T(8,128)(2,1)} %up.1, bf16[896,1024]{1,0:T(8,128)(2,1)} %down.1), custom_call_target="tpu_custom_call" | custom-call | tf_op jit(solution)/shard_map/pack/pallas_call | solution.py:104
  5.4 2.1 collective-permute-start.6
  7.5 2.0 collective-permute-start.7
  9.7 1.6 collective-permute-start
  11.2 1.7 collective-permute-start.1
  13.0 1.9 collective-permute-start.2
  15.0 4.5 %collective-permute-done = bf16[4,256,128]{2,1,0:T(8,128)(2,1)S(1)} collective-permute-done((bf16[4,256,128]{2,1,0:T(8,128)(2,1)S(1)}, bf16[4,256,128]{2,1,0:T(8,128)(2,1)S(1)}, u32[]{:S(2)}, u32[]{:S(2)}) %collective-permute-start) | collective-permute-done | bytes 262176 | tf_op jit(solution)/shard_map/ppermute | solution.py:29
  19.5 0.9 collective-permute-done.1
  20.4 1.4 collective-permute-start.21
  21.8 14.0 %collective-permute-done.6.refs_1_ = bf16[12,128,384]{2,1,0:T(8,128)(2,1)S(1)} collective-permute-done((bf16[12,128,384]{2,1,0:T(8,128)(2,1)}, bf16[12,128,384]{2,1,0:T(8,128)(2,1)S(1)}, u32[]{:S(2)}, u32[]{:S(2)}) %collective-permute-start.6) | collective-permute-done | bytes 1179680 | tf_op jit(solution)/shard_map/ppermute | solution.py:29
  35.8 3.0 collective-permute-start.22
  39.6 1.0 collective-permute-start.8
  40.6 2.3 collective-permute-start.9
  42.9 6.6 %collective-permute-done.22 = bf16[4,256,128]{2,1,0:T(8,128)(2,1)S(1)} collective-permute-done((bf16[4,256,128]{2,1,0:T(8,128)(2,1)S(1)}, bf16[4,256,128]{2,1,0:T(8,128)(2,1)S(1)}, u32[]{:S(2)}, u32[]{:S(2)}) %collective-permute-start.22) | collective-permute-done | bytes 262176 | tf_op jit(solution)/shard_map/ppermute | solution.py:29
  50.3 1.7 collective-permute-start.3
  52.0 2.9 collective-permute-done.8.refs_3_
  55.0 1.1 collective-permute-start.4
  56.1 1.9 collective-permute-start.5
  59.5 7.9 %plan.1.table = s32[8,128]{1,0:T(8,128)} custom-call(s32[64,112]{1,0:T(8,128)} %mask.5, s32[4]{0:T(128)} %pad_add_fusion.where), custom_call_target="tpu_custom_call" | custom-call | tf_op jit(solution)/shard_map/plan/pallas_call | solution.py:162
  67.5 1.0 constant_dynamic-update-slice_fusion.9
  68.5 1.0 constant_dynamic-update-slice_fusion.8
  69.5 1.0 constant_dynamic-update-slice_fusion.7.refs_0_
  70.5 1.5 collective-permute-start.24
  72.0 1.8 collective-permute-start.25
  73.8 7.5 %stage.1.refs_4_ = bf16[97,128,384]{2,1,0:T(8,128)(2,1)} custom-call(bf16[12,128,384]{2,1,0:T(8,128)(2,1)} %pack.1.refs_0_, bf16[12,128,384]{2,1,0:T(8,128)(2,1)} %copy-done.22, bf16[12,128,384]{2,1,0:T(8,128)(2,1)} %copy-done.23, bf16[6,128,384]{2,1,0:T(8,128)(2,1)} %collective-permute-done.8.refs_3_, bf16[6,128,384]{2,1,0:T(8,128)(2,1)} %collective-permute-done.9.refs_4_, ...), custom_call_target="tpu_custom_call" | custom-call | tf_op jit(solution)/shard_map/stage/pallas_call | solution.py:254
  81.4 1.0 copy-done.19
  82.3 1.8 collective-permute-start.26
  84.2 17.3 %collective-permute-done.5.refs_3_ = bf16[16,256,128]{2,1,0:T(8,128)(2,1)} collective-permute-done((bf16[16,256,128]{2,1,0:T(8,128)(2,1)S(1)}, bf16[16,256,128]{2,1,0:T(8,128)(2,1)}, u32[]{:S(2)}, u32[]{:S(2)}) %collective-permute-start.5) | collective-permute-done | bytes 1048608 | tf_op jit(solution)/shard_map/ppermute | solution.py:29
  101.5 3.7 %copy-done = bf16[97,128,384]{2,1,0:T(8,128)(2,1)S(1)} copy-done((bf16[97,128,384]{2,1,0:T(8,128)(2,1)S(1)}, bf16[97,128,384]{2,1,0:T(8,128)(2,1)}, u32[]{:S(2)}) %copy-start) | copy-done | bytes 9535512
  105.2 1.2 copy-done.20
  106.4 10.3 %forward.1 = (bf16[16,256,128]{2,1,0:T(8,128)(2,1)S(1)}, bf16[16,256,128]{2,1,0:T(8,128)(2,1)S(1)}, bf16[16,256,128]{2,1,0:T(8,128)(2,1)S(1)}, bf16[16,256,128]{...) custom-call(s32[8,128]{1,0:T(8,128)S(1)} %copy-done.14, ...), custom_call_target="tpu_custom_call" | custom-call | flops 45097156608 | bytes 20971520 | tf_op jit(solution)/shard_map/forward/pallas_call | solution.py:323
  116.8 2.1 collective-permute-done.25.refs_2_
  118.9 1.8 collective-permute-done.26.refs_3_
  120.7 13.4 %inputs.1 = (bf16[16,256,128]{2,1,0:T(8,128)(2,1)S(1)}, bf16[16,256,128]{2,1,0:T(8,128)(2,1)}, bf16[16,256,128]{2,1,0:T(8,128)(2,1)}, bf16[16,256,128]{2,1,0:T(8...) custom-call(s32[8,128]{1,0:T(8,128)S(1)} %copy-done.14, ...), custom_call_target="tpu_custom_call" | custom-call | flops 60129542144 | bytes 23068672 | tf_op jit(solution)/shard_map/inputs/pallas_call | solution.py:395
  134.1 7.7 %grads.1 = (bf16[12,128,256]{2,1,0:T(8,128)(2,1)S(1)}, bf16[12,128,256]{2,1,0:T(8,128)(2,1)S(1)}, bf16[12,128,256]{2,1,0:T(8,128)(2,1)S(1)}, bf16[12,128,256]{2,1,0:T(8,128)(2,1)S(1)}, bf16[48,128,256]{2,1,0:T(8,128)(2,1)}) custom-call(s32[8,128]{1,0:T(8,128)S(1)} %copy-done.14, bf16[7,256,256]{2,1,0:T(8,128)(2,1)S(1)} %get-tuple-element.47.gucot, ...), custom_call_target="tpu_custom_call" | custom-call | flops 30064771072 | bytes 10485760 | tf_op jit(solution)/shard_map/grads/pallas_call | solution.py:437
  141.9 0.9 copy-done.2
  142.8 0.9 copy-done.4
  143.7 0.9 copy-done.6
  144.6 1.5 collective-permute-start.17
  146.0 1.1 collective-permute-start.16
  147.1 2.2 collective-permute-start.15
  149.3 0.9 collective-permute-start.29
  150.2 22.1 %collective-permute-done.17 = bf16[16,256,128]{2,1,0:T(8,128)(2,1)} collective-permute-done((bf16[16,256,128]{2,1,0:T(8,128)(2,1)S(1)}, bf16[16,256,128]{2,1,0:T(8,128)(2,1)}, u32[]{:S(2)}, u32[]{:S(2)}) %collective-permute-start.17) | collective-permute-done | bytes 1048608 | tf_op jit(solution)/shard_map/ppermute | solution.py:29
  172.3 21.9 %collective-permute-done.16 = bf16[16,256,128]{2,1,0:T(8,128)(2,1)} collective-permute-done((bf16[16,256,128]{2,1,0:T(8,128)(2,1)S(1)}, bf16[16,256,128]{2,1,0:T(8,128)(2,1)}, u32[]{:S(2)}, u32[]{:S(2)}) %collective-permute-start.16) | collective-permute-done | bytes 1048608 | tf_op jit(solution)/shard_map/ppermute | solution.py:29
  194.2 0.9 collective-permute-start.27
  195.1 2.6 zeros.1
  197.7 2.0 add_convert_fusion.16
  199.7 1.1 collective-permute-start.20
  201.0 19.5 %collective-permute-done.27 = bf16[16,256,128]{2,1,0:T(8,128)(2,1)} collective-permute-done((bf16[16,256,128]{2,1,0:T(8,128)(2,1)}, bf16[16,256,128]{2,1,0:T(8,128)(2,1)}, u32[]{:S(2)}, u32[]{:S(2)}) %collective-permute-start.27) | collective-permute-done | bytes 1048608 | tf_op jit(solution)/shard_map/ppermute | solution.py:29
  220.6 1.5 collective-permute-start.18
  222.0 2.0 add_convert_fusion.11
  224.1 1.7 collective-permute-start.32
  225.8 5.0 %collective-permute-done.18 = bf16[4,256,128]{2,1,0:T(8,128)(2,1)S(1)} collective-permute-done((bf16[4,256,128]{2,1,0:T(8,128)(2,1)S(1)}, bf16[4,256,128]{2,1,0:T(8,128)(2,1)S(1)}, u32[]{:S(2)}, u32[]{:S(2)}) %collective-permute-start.18) | collective-permute-done | bytes 262176 | tf_op jit(solution)/shard_map/ppermute | solution.py:29
  231.0 1.4 add_convert_fusion.13
  232.4 2.8 add_convert_fusion.4
  235.2 2.9 collective-permute-start.34
  238.1 3.9 %add_convert_fusion = (bf16[12,128,256]{2,1,0:T(8,128)(2,1)S(1)}, bf16[12,128,256]{2,1,0:T(8,128)(2,1)S(1)}, bf16[12,128,256]{2,1,0:T(8,128)(2,1)S(1)}, bf16[12,128,256]{2,1,0:T(8,128)(2,1)}) fusion(bf16[12,128,256]{2,1,0:T(8,128)(2,1)S(1)} %copy-done.7, bf16[48,128,256]{2,1,0:T(8,128)(2,1)} %collective-permute-done.37, bf16[12,128,256]{2,1,0:T(8,128)(2,1)S(1)} %copy-done.5, ...), kind=kLoop, calls=%fused_computation | loop fusion | flops 6291456 | bytes 9437184 | tf_op jit(solution)/shard_map/convert_element_type | solution.py:53
  242.0 2.0 collective-permute-start.39
  244.0 1.4 add_convert_fusion.8
  245.4 2.2 collective-permute-start.35
  247.6 2.1 collective-permute-start.36
  249.7 0.9 pad_maximum_fusion.1
  250.6 44.5 %collective-permute-done.35.refs_2_ = bf16[12,128,128]{2,1,0:T(8,128)(2,1)S(1)} collective-permute-done((bf16[12,128,128]{2,1,0:T(8,128)(2,1)S(1)}, bf16[12,128,128]{2,1,0:T(8,128)(2,1)S(1)}, u32[]{:S(2)}, u32[]{:S(2)}) %collective-permute-start.35) | collective-permute-done | bytes 393248 | tf_op jit(solution)/shard_map/ppermute | solution.py:29
  296.7 4.4 %unpack.1 = (bf16[1024,896]{1,0:T(8,128)(2,1)}, bf16[1024,896]{1,0:T(8,128)(2,1)}, bf16[896,1024]{1,0:T(8,128)(2,1)}) custom-call(s32[64,112]{1,0:T(8,128)} %mask.5, s32[4]{0:T(128)} %pad_add_fusion.where, bf16[12,128,128]{2,1,0:T(8,128)(2,1)} %get-tuple-element.72.refs_0_, ...), custom_call_target="tpu_custom_call", output_to_operand_aliasing={{0}: (10, {}), {1}: (11, {}), {2}: (12, {})} | custom-call | tf_op jit(solution)/shard_map/unpack/pallas_call | solution.py:513
  (132 shorter events, 6.2 us)
Async XLA Ops:
  1.3 8.2 %copy-start.27 = (bf16[256,512]{1,0:T(8,128)(2,1)S(1)}, bf16[256,512]{1,0:T(8,128)(2,1)}, u32[]{:S(2)}) copy-start(bf16[256,512]{1,0:T(8,128)(2,1)} %param.6) | copy-start | bytes 786436
  1.3 13.6 %copy-start.28 = (bf16[256,512]{1,0:T(8,128)(2,1)S(1)}, bf16[256,512]{1,0:T(8,128)(2,1)}, u32[]{:S(2)}) copy-start(bf16[256,512]{1,0:T(8,128)(2,1)} %param.7) | copy-start | bytes 786436
  5.4 14.1 %copy-start.21 = (bf16[12,128,384]{2,1,0:T(8,128)(2,1)S(1)}, bf16[12,128,384]{2,1,0:T(8,128)(2,1)}, u32[]{:S(2)}) copy-start(bf16[12,128,384]{2,1,0:T(8,128)(2,1)} %pack.1.refs_0_) | copy-start | bytes 3538948
  5.4 30.4 %collective-permute-start.6 = (bf16[12,128,384]{2,1,0:T(8,128)(2,1)}, bf16[12,128,384]{2,1,0:T(8,128)(2,1)S(1)}, u32[]{:S(2)}, u32[]{:S(2)}) collective-permute-start(bf16[12,128,384]{2,1,0:T(8,128)(2,1)} %pack.1.refs_0_), channel_id=1, source_target_pairs={{0,32},{1,33},{2,34},{3,35},{4,36},{5,37},{6,38},{7,39},{8,40},{9,... | collective-permute-start | bytes 3538952 | tf_op jit(solution)/shard_map/ppermute | solution.py:29
  7.5 31.2 %collective-permute-start.7 = (bf16[12,128,384]{2,1,0:T(8,128)(2,1)}, bf16[12,128,384]{2,1,0:T(8,128)(2,1)S(1)}, u32[]{:S(2)}, u32[]{:S(2)}) collective-permute-start(bf16[12,128,384]{2,1,0:T(8,128)(2,1)} %pack.1.refs_0_), channel_id=1, source_target_pairs={{0,96},{1,97},{2,98},{3,99},{4,100},{5,101},{6,102},{7,103},{8,104... | collective-permute-start | bytes 3538952 | tf_op jit(solution)/shard_map/ppermute | solution.py:29
  9.7 9.8 %collective-permute-start = (bf16[4,256,128]{2,1,0:T(8,128)(2,1)S(1)}, bf16[4,256,128]{2,1,0:T(8,128)(2,1)S(1)}, u32[]{:S(2)}, u32[]{:S(2)}) collective-permute-start(bf16[4,256,128]{2,1,0:T(8,128)(2,1)S(1)} %pad_maximum_fusion), channel_id=1, source_target_pairs={{0,4},{1,5},{2,6},{3,7},{4,8},{5,9},{6,10},{7,11},{8,12},{9,13},{1... | collective-permute-start | bytes 786440 | tf_op jit(solution)/shard_map/ppermute | solution.py:29
  11.2 9.2 %collective-permute-start.1 = (bf16[4,256,128]{2,1,0:T(8,128)(2,1)S(1)}, bf16[4,256,128]{2,1,0:T(8,128)(2,1)S(1)}, u32[]{:S(2)}, u32[]{:S(2)}) collective-permute-start(bf16[4,256,128]{2,1,0:T(8,128)(2,1)S(1)} %pad_maximum_fusion), channel_id=1, source_target_pairs={{0,12},{1,13},{2,14},{3,15},{4,0},{5,1},{6,2},{7,3},{8,4},{9,5},{1... | collective-permute-start | bytes 786440 | tf_op jit(solution)/shard_map/ppermute | solution.py:29
  13.0 26.6 %collective-permute-start.2 = (bf16[4,256,128]{2,1,0:T(8,128)(2,1)S(1)}, bf16[4,256,128]{2,1,0:T(8,128)(2,1)S(1)}, u32[]{:S(2)}, u32[]{:S(2)}) collective-permute-start(bf16[4,256,128]{2,1,0:T(8,128)(2,1)S(1)} %pad_maximum_fusion), channel_id=1, source_target_pairs={{0,8},{1,9},{2,10},{3,11},{4,12},{5,13},{6,14},{7,15},{8,0},{9,1},... | collective-permute-start | bytes 786440 | tf_op jit(solution)/shard_map/ppermute | solution.py:29
  19.5 30.8 %collective-permute-start.10 = (bf16[12,128,384]{2,1,0:T(8,128)(2,1)S(1)}, bf16[12,128,384]{2,1,0:T(8,128)(2,1)S(1)}, u32[]{:S(2)}, u32[]{:S(2)}) collective-permute-start(bf16[12,128,384]{2,1,0:T(8,128)(2,1)S(1)} %copy-done.21), channel_id=1, source_target_pairs={{0,16},{1,17},{2,18},{3,19},{4,20},{5,21},{6,22},{7,23},{8,24},{9,... | collective-permute-start | bytes 3538952 | tf_op jit(solution)/shard_map/ppermute | solution.py:29
  20.4 20.2 %collective-permute-start.21 = (bf16[4,256,128]{2,1,0:T(8,128)(2,1)S(1)}, bf16[4,256,128]{2,1,0:T(8,128)(2,1)S(1)}, u32[]{:S(2)}, u32[]{:S(2)}) collective-permute-start(bf16[4,256,128]{2,1,0:T(8,128)(2,1)S(1)} %pad_maximum_fusion.2), channel_id=1, source_target_pairs={{0,1},{1,2},{2,3},{3,0},{4,5},{5,6},{6,7},{7,4},{8,9},{9,10},{10,1... | collective-permute-start | bytes 786440 | tf_op jit(solution)/shard_map/ppermute | solution.py:29
  35.8 14.3 %copy-start.22 = (bf16[12,128,384]{2,1,0:T(8,128)(2,1)}, bf16[12,128,384]{2,1,0:T(8,128)(2,1)S(1)}, u32[]{:S(2)}) copy-start(bf16[12,128,384]{2,1,0:T(8,128)(2,1)S(1)} %collective-permute-done.6.refs_1_) | copy-start | bytes 3538948
  35.8 13.7 %collective-permute-start.22 = (bf16[4,256,128]{2,1,0:T(8,128)(2,1)S(1)}, bf16[4,256,128]{2,1,0:T(8,128)(2,1)S(1)}, u32[]{:S(2)}, u32[]{:S(2)}) collective-permute-start(bf16[4,256,128]{2,1,0:T(8,128)(2,1)S(1)} %pad_maximum_fusion.2), channel_id=1, source_target_pairs={{0,3},{1,0},{2,1},{3,2},{4,7},{5,4},{6,5},{7,6},{8,11},{9,8},{10,9... | collective-permute-start | bytes 786440 | tf_op jit(solution)/shard_map/ppermute | solution.py:29
  38.8 11.3 %copy-start.23 = (bf16[12,128,384]{2,1,0:T(8,128)(2,1)}, bf16[12,128,384]{2,1,0:T(8,128)(2,1)S(1)}, u32[]{:S(2)}) copy-start(bf16[12,128,384]{2,1,0:T(8,128)(2,1)S(1)} %collective-permute-done.7.refs_2_) | copy-start | bytes 3538948
  38.8 10.7 %collective-permute-start.23 = (bf16[4,256,128]{2,1,0:T(8,128)(2,1)S(1)}, bf16[4,256,128]{2,1,0:T(8,128)(2,1)S(1)}, u32[]{:S(2)}, u32[]{:S(2)}) collective-permute-start(bf16[4,256,128]{2,1,0:T(8,128)(2,1)S(1)} %pad_maximum_fusion.2), channel_id=1, source_target_pairs={{0,2},{1,3},{2,0},{3,1},{4,6},{5,7},{6,4},{7,5},{8,10},{9,11},{10,... | collective-permute-start | bytes 786440 | tf_op jit(solution)/shard_map/ppermute | solution.py:29
  39.6 15.4 %collective-permute-start.8 = (bf16[6,128,384]{2,1,0:T(8,128)(2,1)S(1)}, bf16[6,128,384]{2,1,0:T(8,128)(2,1)}, u32[]{:S(2)}, u32[]{:S(2)}) collective-permute-start(bf16[6,128,384]{2,1,0:T(8,128)(2,1)S(1)} %slice.232), channel_id=1, source_target_pairs={{0,32},{1,33},{2,34},{3,35},{4,36},{5,37},{6,38},{7,39},{8,40},{9,... | collective-permute-start | bytes 1769480 | tf_op jit(solution)/shard_map/ppermute | solution.py:29
  40.6 15.5 %copy-start.35 = (bf16[4,256,128]{2,1,0:T(8,128)(2,1)}, bf16[4,256,128]{2,1,0:T(8,128)(2,1)S(1)}, u32[]{:S(2)}) copy-start(bf16[4,256,128]{2,1,0:T(8,128)(2,1)S(1)} %collective-permute-done.21) | copy-start | bytes 786436
  40.6 15.5 %collective-permute-start.9 = (bf16[6,128,384]{2,1,0:T(8,128)(2,1)S(1)}, bf16[6,128,384]{2,1,0:T(8,128)(2,1)}, u32[]{:S(2)}, u32[]{:S(2)}) collective-permute-start(bf16[6,128,384]{2,1,0:T(8,128)(2,1)S(1)} %slice.233), channel_id=1, source_target_pairs={{0,96},{1,97},{2,98},{3,99},{4,100},{5,101},{6,102},{7,103},{8,104... | collective-permute-start | bytes 1769480 | tf_op jit(solution)/shard_map/ppermute | solution.py:29
  49.5 8.6 %collective-permute-start.11 = (bf16[12,128,384]{2,1,0:T(8,128)(2,1)S(1)}, bf16[12,128,384]{2,1,0:T(8,128)(2,1)S(1)}, u32[]{:S(2)}, u32[]{:S(2)}) collective-permute-start(bf16[12,128,384]{2,1,0:T(8,128)(2,1)S(1)} %collective-permute-done.6.refs_1_), channel_id=1, source_target_pairs={{0,16},{1,17},{2,18},{3,19},{4,20},{5,21},{6,22},{7,23},{8,24},{9,... | collective-permute-start | bytes 3538952 | tf_op jit(solution)/shard_map/ppermute | solution.py:29
  49.5 8.7 %collective-permute-start.12 = (bf16[12,128,384]{2,1,0:T(8,128)(2,1)S(1)}, bf16[12,128,384]{2,1,0:T(8,128)(2,1)S(1)}, u32[]{:S(2)}, u32[]{:S(2)}) collective-permute-start(bf16[12,128,384]{2,1,0:T(8,128)(2,1)S(1)} %collective-permute-done.7.refs_2_), channel_id=1, source_target_pairs={{0,16},{1,17},{2,18},{3,19},{4,20},{5,21},{6,22},{7,23},{8,24},{9,... | collective-permute-start | bytes 3538952 | tf_op jit(solution)/shard_map/ppermute | solution.py:29
  50.3 51.2 %copy-start.15 = (bf16[16,256,128]{2,1,0:T(8,128)(2,1)}, bf16[16,256,128]{2,1,0:T(8,128)(2,1)S(1)}, u32[]{:S(2)}) copy-start(bf16[16,256,128]{2,1,0:T(8,128)(2,1)S(1)} %constant_dynamic-update-slice_fusion.refs_0_) | copy-start | bytes 3145732
  50.3 7.9 %copy-start.24 = (bf16[12,128,384]{2,1,0:T(8,128)(2,1)}, bf16[12,128,384]{2,1,0:T(8,128)(2,1)S(1)}, u32[]{:S(2)}) copy-start(bf16[12,128,384]{2,1,0:T(8,128)(2,1)S(1)} %collective-permute-done.10.refs_5_) | copy-start | bytes 3538948
  50.3 31.0 %collective-permute-start.3 = (bf16[16,256,128]{2,1,0:T(8,128)(2,1)S(1)}, bf16[16,256,128]{2,1,0:T(8,128)(2,1)S(1)}, u32[]{:S(2)}, u32[]{:S(2)}) collective-permute-start(bf16[16,256,128]{2,1,0:T(8,128)(2,1)S(1)} %constant_dynamic-update-slice_fusion.refs_0_), channel_id=1, source_target_pairs={{0,1},{1,2},{2,3},{3,0},{4,5},{5,6},{6,7},{7,4},{8,9},{9,10},{10,1... | collective-permute-start | bytes 3145736 | tf_op jit(solution)/shard_map/ppermute | solution.py:29
  55.0 29.2 %collective-permute-start.4 = (bf16[16,256,128]{2,1,0:T(8,128)(2,1)S(1)}, bf16[16,256,128]{2,1,0:T(8,128)(2,1)}, u32[]{:S(2)}, u32[]{:S(2)}) collective-permute-start(bf16[16,256,128]{2,1,0:T(8,128)(2,1)S(1)} %constant_dynamic-update-slice_fusion.refs_0_), channel_id=1, source_target_pairs={{0,3},{1,0},{2,1},{3,2},{4,7},{5,4},{6,5},{7,6},{8,11},{9,8},{10,9... | collective-permute-start | bytes 3145736 | tf_op jit(solution)/shard_map/ppermute | solution.py:29
  56.1 45.4 %collective-permute-start.5 = (bf16[16,256,128]{2,1,0:T(8,128)(2,1)S(1)}, bf16[16,256,128]{2,1,0:T(8,128)(2,1)}, u32[]{:S(2)}, u32[]{:S(2)}) collective-permute-start(bf16[16,256,128]{2,1,0:T(8,128)(2,1)S(1)} %constant_dynamic-update-slice_fusion.refs_0_), channel_id=1, source_target_pairs={{0,2},{1,3},{2,0},{3,1},{4,6},{5,7},{6,4},{7,5},{8,10},{9,11},{10,... | collective-permute-start | bytes 3145736 | tf_op jit(solution)/shard_map/ppermute | solution.py:29
  58.1 12.4 %collective-permute-start.13 = (bf16[6,128,384]{2,1,0:T(8,128)(2,1)}, bf16[6,128,384]{2,1,0:T(8,128)(2,1)}, u32[]{:S(2)}, u32[]{:S(2)}) collective-permute-start(bf16[6,128,384]{2,1,0:T(8,128)(2,1)} %collective-permute-done.8.refs_3_), channel_id=1, source_target_pairs={{0,16},{1,17},{2,18},{3,19},{4,20},{5,21},{6,22},{7,23},{8,24},{9,... | collective-permute-start | bytes 1769480 | tf_op jit(solution)/shard_map/ppermute | solution.py:29
  58.2 13.8 %collective-permute-start.14 = (bf16[6,128,384]{2,1,0:T(8,128)(2,1)}, bf16[6,128,384]{2,1,0:T(8,128)(2,1)}, u32[]{:S(2)}, u32[]{:S(2)}) collective-permute-start(bf16[6,128,384]{2,1,0:T(8,128)(2,1)} %collective-permute-done.9.refs_4_), channel_id=1, source_target_pairs={{0,16},{1,17},{2,18},{3,19},{4,20},{5,21},{6,22},{7,23},{8,24},{9,... | collective-permute-start | bytes 1769480 | tf_op jit(solution)/shard_map/ppermute | solution.py:29
  70.5 10.8 %copy-start.17 = (bf16[16,256,128]{2,1,0:T(8,128)(2,1)}, bf16[16,256,128]{2,1,0:T(8,128)(2,1)S(1)}, u32[]{:S(2)}) copy-start(bf16[16,256,128]{2,1,0:T(8,128)(2,1)S(1)} %constant_dynamic-update-slice_fusion.7.refs_0_) | copy-start | bytes 3145732
  70.5 31.0 %copy-start.14 = (s32[8,128]{1,0:T(8,128)S(1)}, s32[8,128]{1,0:T(8,128)}, u32[]{:S(2)}) copy-start(s32[8,128]{1,0:T(8,128)} %plan.1.table) | copy-start | bytes 12292
  70.5 46.3 %collective-permute-start.24 = (bf16[16,256,128]{2,1,0:T(8,128)(2,1)S(1)}, bf16[16,256,128]{2,1,0:T(8,128)(2,1)}, u32[]{:S(2)}, u32[]{:S(2)}) collective-permute-start(bf16[16,256,128]{2,1,0:T(8,128)(2,1)S(1)} %constant_dynamic-update-slice_fusion.7.refs_0_), channel_id=1, source_target_pairs={{0,4},{1,5},{2,6},{3,7},{4,8},{5,9},{6,10},{7,11},{8,12},{9,13},{1... | collective-permute-start | bytes 3145736 | tf_op jit(solution)/shard_map/ppermute | solution.py:29
  72.0 46.9 %collective-permute-start.25 = (bf16[16,256,128]{2,1,0:T(8,128)(2,1)S(1)}, bf16[16,256,128]{2,1,0:T(8,128)(2,1)}, u32[]{:S(2)}, u32[]{:S(2)}) collective-permute-start(bf16[16,256,128]{2,1,0:T(8,128)(2,1)S(1)} %constant_dynamic-update-slice_fusion.7.refs_0_), channel_id=1, source_target_pairs={{0,12},{1,13},{2,14},{3,15},{4,0},{5,1},{6,2},{7,3},{8,4},{9,5},{1... | collective-permute-start | bytes 3145736 | tf_op jit(solution)/shard_map/ppermute | solution.py:29
  82.3 38.4 %collective-permute-start.26 = (bf16[16,256,128]{2,1,0:T(8,128)(2,1)S(1)}, bf16[16,256,128]{2,1,0:T(8,128)(2,1)S(1)}, u32[]{:S(2)}, u32[]{:S(2)}) collective-permute-start(bf16[16,256,128]{2,1,0:T(8,128)(2,1)S(1)} %constant_dynamic-update-slice_fusion.7.refs_0_), channel_id=1, source_target_pairs={{0,8},{1,9},{2,10},{3,11},{4,12},{5,13},{6,14},{7,15},{8,0},{9,1},... | collective-permute-start | bytes 3145736 | tf_op jit(solution)/shard_map/ppermute | solution.py:29
  106.4 14.2 %copy-start.1 = (bf16[97,128,384]{2,1,0:T(8,128)(2,1)S(1)}, bf16[97,128,384]{2,1,0:T(8,128)(2,1)}, u32[]{:S(2)}) copy-start(bf16[97,128,384]{2,1,0:T(8,128)(2,1)} %stage.1.refs_4_) | copy-start | bytes 28606468
  106.4 14.2 %copy-start.18 = (bf16[16,256,128]{2,1,0:T(8,128)(2,1)S(1)}, bf16[16,256,128]{2,1,0:T(8,128)(2,1)}, u32[]{:S(2)}) copy-start(bf16[16,256,128]{2,1,0:T(8,128)(2,1)} %copy-done.17) | copy-start | bytes 3145732
  120.7 13.4 %copy-start.16 = (bf16[16,256,128]{2,1,0:T(8,128)(2,1)S(1)}, bf16[16,256,128]{2,1,0:T(8,128)(2,1)}, u32[]{:S(2)}) copy-start(bf16[16,256,128]{2,1,0:T(8,128)(2,1)} %copy-done.15) | copy-start | bytes 3145732
  134.1 7.8 %copy-start.8 = (bf16[12,128,128]{2,1,0:T(8,128)(2,1)}, bf16[12,128,128]{2,1,0:T(8,128)(2,1)S(1)}, u32[]{:S(2)}) copy-start(bf16[12,128,128]{2,1,0:T(8,128)(2,1)S(1)} %get-tuple-element.44) | copy-start | bytes 1179652
  134.1 7.8 %copy-start.10 = (bf16[12,128,128]{2,1,0:T(8,128)(2,1)}, bf16[12,128,128]{2,1,0:T(8,128)(2,1)S(1)}, u32[]{:S(2)}) copy-start(bf16[12,128,128]{2,1,0:T(8,128)(2,1)S(1)} %get-tuple-element.45) | copy-start | bytes 1179652
  134.1 7.8 %copy-start.12 = (bf16[12,128,128]{2,1,0:T(8,128)(2,1)}, bf16[12,128,128]{2,1,0:T(8,128)(2,1)S(1)}, u32[]{:S(2)}) copy-start(bf16[12,128,128]{2,1,0:T(8,128)(2,1)S(1)} %get-tuple-element.46) | copy-start | bytes 1179652
  144.6 93.5 %collective-permute-start.37 = (bf16[48,128,256]{2,1,0:T(8,128)(2,1)}, bf16[48,128,256]{2,1,0:T(8,128)(2,1)}, u32[]{:S(2)}, u32[]{:S(2)}) collective-permute-start(bf16[48,128,256]{2,1,0:T(8,128)(2,1)} %get-tuple-element.49), channel_id=1, source_target_pairs={{0,16},{1,17},{2,18},{3,19},{4,20},{5,21},{6,22},{7,23},{8,24},{9,... | collective-permute-start | bytes 9437192 | tf_op jit(solution)/shard_map/ppermute | solution.py:29
  144.6 27.7 %collective-permute-start.17 = (bf16[16,256,128]{2,1,0:T(8,128)(2,1)S(1)}, bf16[16,256,128]{2,1,0:T(8,128)(2,1)}, u32[]{:S(2)}, u32[]{:S(2)}) collective-permute-start(bf16[16,256,128]{2,1,0:T(8,128)(2,1)S(1)} %get-tuple-element.35), channel_id=1, source_target_pairs={{0,2},{1,3},{2,0},{3,1},{4,6},{5,7},{6,4},{7,5},{8,10},{9,11},{10,... | collective-permute-start | bytes 3145736 | tf_op jit(solution)/shard_map/ppermute | solution.py:29
  146.0 48.2 %collective-permute-start.16 = (bf16[16,256,128]{2,1,0:T(8,128)(2,1)S(1)}, bf16[16,256,128]{2,1,0:T(8,128)(2,1)}, u32[]{:S(2)}, u32[]{:S(2)}) collective-permute-start(bf16[16,256,128]{2,1,0:T(8,128)(2,1)S(1)} %get-tuple-element.34), channel_id=1, source_target_pairs={{0,1},{1,2},{2,3},{3,0},{4,5},{5,6},{6,7},{7,4},{8,9},{9,10},{10,1... | collective-permute-start | bytes 3145736 | tf_op jit(solution)/shard_map/ppermute | solution.py:29
  147.1 48.0 %collective-permute-start.15 = (bf16[16,256,128]{2,1,0:T(8,128)(2,1)S(1)}, bf16[16,256,128]{2,1,0:T(8,128)(2,1)}, u32[]{:S(2)}, u32[]{:S(2)}) collective-permute-start(bf16[16,256,128]{2,1,0:T(8,128)(2,1)S(1)} %get-tuple-element.33), channel_id=1, source_target_pairs={{0,3},{1,0},{2,1},{3,2},{4,7},{5,4},{6,5},{7,6},{8,11},{9,8},{10,9... | collective-permute-start | bytes 3145736 | tf_op jit(solution)/shard_map/ppermute | solution.py:29
  149.3 50.4 %collective-permute-start.29 = (bf16[16,256,128]{2,1,0:T(8,128)(2,1)}, bf16[16,256,128]{2,1,0:T(8,128)(2,1)}, u32[]{:S(2)}, u32[]{:S(2)}) collective-permute-start(bf16[16,256,128]{2,1,0:T(8,128)(2,1)} %get-tuple-element.41), channel_id=1, source_target_pairs={{0,8},{1,9},{2,10},{3,11},{4,12},{5,13},{6,14},{7,15},{8,0},{9,1},... | collective-permute-start | bytes 3145736 | tf_op jit(solution)/shard_map/ppermute | solution.py:29
  172.3 28.5 %collective-permute-start.28 = (bf16[16,256,128]{2,1,0:T(8,128)(2,1)}, bf16[16,256,128]{2,1,0:T(8,128)(2,1)}, u32[]{:S(2)}, u32[]{:S(2)}) collective-permute-start(bf16[16,256,128]{2,1,0:T(8,128)(2,1)} %get-tuple-element.40), channel_id=1, source_target_pairs={{0,4},{1,5},{2,6},{3,7},{4,8},{5,9},{6,10},{7,11},{8,12},{9,13},{1... | collective-permute-start | bytes 3145736 | tf_op jit(solution)/shard_map/ppermute | solution.py:29
  194.2 26.3 %collective-permute-start.27 = (bf16[16,256,128]{2,1,0:T(8,128)(2,1)}, bf16[16,256,128]{2,1,0:T(8,128)(2,1)}, u32[]{:S(2)}, u32[]{:S(2)}) collective-permute-start(bf16[16,256,128]{2,1,0:T(8,128)(2,1)} %get-tuple-element.39), channel_id=1, source_target_pairs={{0,12},{1,13},{2,14},{3,15},{4,0},{5,1},{6,2},{7,3},{8,4},{9,5},{1... | collective-permute-start | bytes 3145736 | tf_op jit(solution)/shard_map/ppermute | solution.py:29
  195.1 37.3 %collective-permute-start.33 = (bf16[48,128,128]{2,1,0:T(8,128)(2,1)}, bf16[48,128,128]{2,1,0:T(8,128)(2,1)}, u32[]{:S(2)}, u32[]{:S(2)}) collective-permute-start(bf16[48,128,128]{2,1,0:T(8,128)(2,1)} %get-tuple-element.43), channel_id=1, source_target_pairs={{0,16},{1,17},{2,18},{3,19},{4,20},{5,21},{6,22},{7,23},{8,24},{9,... | collective-permute-start | bytes 4718600 | tf_op jit(solution)/shard_map/ppermute | solution.py:29
  199.7 24.4 %collective-permute-start.20 = (bf16[4,256,128]{2,1,0:T(8,128)(2,1)S(1)}, bf16[4,256,128]{2,1,0:T(8,128)(2,1)S(1)}, u32[]{:S(2)}, u32[]{:S(2)}) collective-permute-start(bf16[4,256,128]{2,1,0:T(8,128)(2,1)S(1)} %get-tuple-element.63), channel_id=1, source_target_pairs={{0,8},{1,9},{2,10},{3,11},{4,12},{5,13},{6,14},{7,15},{8,0},{9,1},... | collective-permute-start | bytes 786440 | tf_op jit(solution)/shard_map/ppermute | solution.py:29
  200.8 25.1 %collective-permute-start.19 = (bf16[4,256,128]{2,1,0:T(8,128)(2,1)S(1)}, bf16[4,256,128]{2,1,0:T(8,128)(2,1)S(1)}, u32[]{:S(2)}, u32[]{:S(2)}) collective-permute-start(bf16[4,256,128]{2,1,0:T(8,128)(2,1)S(1)} %get-tuple-element.64), channel_id=1, source_target_pairs={{0,4},{1,5},{2,6},{3,7},{4,8},{5,9},{6,10},{7,11},{8,12},{9,13},{1... | collective-permute-start | bytes 786440 | tf_op jit(solution)/shard_map/ppermute | solution.py:29
  220.6 10.3 %collective-permute-start.18 = (bf16[4,256,128]{2,1,0:T(8,128)(2,1)S(1)}, bf16[4,256,128]{2,1,0:T(8,128)(2,1)S(1)}, u32[]{:S(2)}, u32[]{:S(2)}) collective-permute-start(bf16[4,256,128]{2,1,0:T(8,128)(2,1)S(1)} %get-tuple-element.62), channel_id=1, source_target_pairs={{0,12},{1,13},{2,14},{3,15},{4,0},{5,1},{6,2},{7,3},{8,4},{9,5},{1... | collective-permute-start | bytes 786440 | tf_op jit(solution)/shard_map/ppermute | solution.py:29
  224.1 8.3 %copy-start.9 = (bf16[12,128,128]{2,1,0:T(8,128)(2,1)S(1)}, bf16[12,128,128]{2,1,0:T(8,128)(2,1)}, u32[]{:S(2)}) copy-start(bf16[12,128,128]{2,1,0:T(8,128)(2,1)} %copy-done.8) | copy-start | bytes 1179652
  224.1 8.3 %copy-start.11 = (bf16[12,128,128]{2,1,0:T(8,128)(2,1)S(1)}, bf16[12,128,128]{2,1,0:T(8,128)(2,1)}, u32[]{:S(2)}) copy-start(bf16[12,128,128]{2,1,0:T(8,128)(2,1)} %copy-done.10) | copy-start | bytes 1179652
  224.1 8.3 %copy-start.13 = (bf16[12,128,128]{2,1,0:T(8,128)(2,1)S(1)}, bf16[12,128,128]{2,1,0:T(8,128)(2,1)}, u32[]{:S(2)}) copy-start(bf16[12,128,128]{2,1,0:T(8,128)(2,1)} %copy-done.12) | copy-start | bytes 1179652
  224.1 17.9 %collective-permute-start.32 = (bf16[4,256,128]{2,1,0:T(8,128)(2,1)S(1)}, bf16[4,256,128]{2,1,0:T(8,128)(2,1)S(1)}, u32[]{:S(2)}, u32[]{:S(2)}) collective-permute-start(bf16[4,256,128]{2,1,0:T(8,128)(2,1)S(1)} %get-tuple-element.60), channel_id=1, source_target_pairs={{0,2},{1,3},{2,0},{3,1},{4,6},{5,7},{6,4},{7,5},{8,10},{9,11},{10,... | collective-permute-start | bytes 786440 | tf_op jit(solution)/shard_map/ppermute | solution.py:29
  225.8 18.2 %collective-permute-start.31 = (bf16[4,256,128]{2,1,0:T(8,128)(2,1)S(1)}, bf16[4,256,128]{2,1,0:T(8,128)(2,1)S(1)}, u32[]{:S(2)}, u32[]{:S(2)}) collective-permute-start(bf16[4,256,128]{2,1,0:T(8,128)(2,1)S(1)} %get-tuple-element.61), channel_id=1, source_target_pairs={{0,1},{1,2},{2,3},{3,0},{4,5},{5,6},{6,7},{7,4},{8,9},{9,10},{10,1... | collective-permute-start | bytes 786440 | tf_op jit(solution)/shard_map/ppermute | solution.py:29
  230.8 13.2 %collective-permute-start.30 = (bf16[4,256,128]{2,1,0:T(8,128)(2,1)S(1)}, bf16[4,256,128]{2,1,0:T(8,128)(2,1)S(1)}, u32[]{:S(2)}, u32[]{:S(2)}) collective-permute-start(bf16[4,256,128]{2,1,0:T(8,128)(2,1)S(1)} %get-tuple-element.59), channel_id=1, source_target_pairs={{0,3},{1,0},{2,1},{3,2},{4,7},{5,4},{6,5},{7,6},{8,11},{9,8},{10,9... | collective-permute-start | bytes 786440 | tf_op jit(solution)/shard_map/ppermute | solution.py:29
  232.4 5.7 %copy-start.3 = (bf16[12,128,256]{2,1,0:T(8,128)(2,1)S(1)}, bf16[12,128,256]{2,1,0:T(8,128)(2,1)}, u32[]{:S(2)}) copy-start(bf16[12,128,256]{2,1,0:T(8,128)(2,1)} %copy-done.2) | copy-start | bytes 2359300
  232.4 5.7 %copy-start.5 = (bf16[12,128,256]{2,1,0:T(8,128)(2,1)S(1)}, bf16[12,128,256]{2,1,0:T(8,128)(2,1)}, u32[]{:S(2)}) copy-start(bf16[12,128,256]{2,1,0:T(8,128)(2,1)} %copy-done.4) | copy-start | bytes 2359300
  232.4 5.7 %copy-start.7 = (bf16[12,128,256]{2,1,0:T(8,128)(2,1)S(1)}, bf16[12,128,256]{2,1,0:T(8,128)(2,1)}, u32[]{:S(2)}) copy-start(bf16[12,128,256]{2,1,0:T(8,128)(2,1)} %copy-done.6) | copy-start | bytes 2359300
  235.2 12.4 %collective-permute-start.34 = (bf16[12,128,128]{2,1,0:T(8,128)(2,1)S(1)}, bf16[12,128,128]{2,1,0:T(8,128)(2,1)S(1)}, u32[]{:S(2)}, u32[]{:S(2)}) collective-permute-start(bf16[12,128,128]{2,1,0:T(8,128)(2,1)S(1)} %get-tuple-element.71), channel_id=1, source_target_pairs={{0,96},{1,97},{2,98},{3,99},{4,100},{5,101},{6,102},{7,103},{8,104... | collective-permute-start | bytes 1179656 | tf_op jit(solution)/shard_map/ppermute | solution.py:29
  242.0 53.1 %collective-permute-start.38 = (bf16[12,128,256]{2,1,0:T(8,128)(2,1)S(1)}, bf16[12,128,256]{2,1,0:T(8,128)(2,1)S(1)}, u32[]{:S(2)}, u32[]{:S(2)}) collective-permute-start(bf16[12,128,256]{2,1,0:T(8,128)(2,1)S(1)} %get-tuple-element.67), channel_id=1, source_target_pairs={{0,96},{1,97},{2,98},{3,99},{4,100},{5,101},{6,102},{7,103},{8,104... | collective-permute-start | bytes 2359304 | tf_op jit(solution)/shard_map/ppermute | solution.py:29
  242.0 53.1 %collective-permute-start.39 = (bf16[12,128,256]{2,1,0:T(8,128)(2,1)S(1)}, bf16[12,128,256]{2,1,0:T(8,128)(2,1)S(1)}, u32[]{:S(2)}, u32[]{:S(2)}) collective-permute-start(bf16[12,128,256]{2,1,0:T(8,128)(2,1)S(1)} %get-tuple-element.66), channel_id=1, source_target_pairs={{0,32},{1,33},{2,34},{3,35},{4,36},{5,37},{6,38},{7,39},{8,40},{9,... | collective-permute-start | bytes 2359304 | tf_op jit(solution)/shard_map/ppermute | solution.py:29
  244.0 51.1 %collective-permute-start.40 = (bf16[12,128,256]{2,1,0:T(8,128)(2,1)S(1)}, bf16[12,128,256]{2,1,0:T(8,128)(2,1)S(1)}, u32[]{:S(2)}, u32[]{:S(2)}) collective-permute-start(bf16[12,128,256]{2,1,0:T(8,128)(2,1)S(1)} %get-tuple-element.65), channel_id=1, source_target_pairs={{0,64},{1,65},{2,66},{3,67},{4,68},{5,69},{6,70},{7,71},{8,72},{9,... | collective-permute-start | bytes 2359304 | tf_op jit(solution)/shard_map/ppermute | solution.py:29
  245.4 49.7 %collective-permute-start.35 = (bf16[12,128,128]{2,1,0:T(8,128)(2,1)S(1)}, bf16[12,128,128]{2,1,0:T(8,128)(2,1)S(1)}, u32[]{:S(2)}, u32[]{:S(2)}) collective-permute-start(bf16[12,128,128]{2,1,0:T(8,128)(2,1)S(1)} %get-tuple-element.70), channel_id=1, source_target_pairs={{0,32},{1,33},{2,34},{3,35},{4,36},{5,37},{6,38},{7,39},{8,40},{9,... | collective-permute-start | bytes 1179656 | tf_op jit(solution)/shard_map/ppermute | solution.py:29
  247.6 47.5 %copy-start.32 = (bf16[12,128,128]{2,1,0:T(8,128)(2,1)}, bf16[12,128,128]{2,1,0:T(8,128)(2,1)S(1)}, u32[]{:S(2)}) copy-start(bf16[12,128,128]{2,1,0:T(8,128)(2,1)S(1)} %collective-permute-done.34.refs_1_) | copy-start | bytes 1179652
  247.6 47.4 %collective-permute-start.36 = (bf16[12,128,128]{2,1,0:T(8,128)(2,1)S(1)}, bf16[12,128,128]{2,1,0:T(8,128)(2,1)S(1)}, u32[]{:S(2)}, u32[]{:S(2)}) collective-permute-start(bf16[12,128,128]{2,1,0:T(8,128)(2,1)S(1)} %get-tuple-element.69), channel_id=1, source_target_pairs={{0,64},{1,65},{2,66},{3,67},{4,68},{5,69},{6,70},{7,71},{8,72},{9,... | collective-permute-start | bytes 1179656 | tf_op jit(solution)/shard_map/ppermute | solution.py:29
  (15 other events, 18.3 us)

commit v2 on v1

--- a/solution.py
+++ b/solution.py
@@ -100,13 +100,14 @@
 
 def pack(mask, where, gate, up, down):
     smem = pl.BlockSpec(memory_space=pltpu.SMEM)
-    hbm = pl.BlockSpec(memory_space=pl.ANY)
+    hbm = pl.BlockSpec(memory_space=pltpu.HBM)
     return pl.pallas_call(
         pack_body,
         out_shape=jax.ShapeDtypeStruct((CAP, BLK, 3 * BLK), BF),
         in_specs=[smem, smem, hbm, hbm, hbm],
         out_specs=pl.BlockSpec(memory_space=pltpu.VMEM),
         scratch_shapes=[pltpu.SemaphoreType.DMA((CAP, 3))],
+        compiler_params=pltpu.CompilerParams(vmem_limit_bytes=4 * MIB),
         name="pack",
     )(mask, where, gate, up, down)
 
@@ -164,6 +165,7 @@
         out_shape=jax.ShapeDtypeStruct((8, 128), jnp.int32),
         in_specs=[smem, smem],
         out_specs=smem,
+        compiler_params=pltpu.CompilerParams(vmem_limit_bytes=2 * MIB),
         name="plan",
     )(mask, where)
 
@@ -257,6 +259,7 @@
         in_specs=[HBM] * 10,
         out_specs=IN_VMEM,
         scratch_shapes=[pltpu.SemaphoreType.DMA((10,))],
+        compiler_params=pltpu.CompilerParams(vmem_limit_bytes=12 * MIB),
         name="stage",
     )(*parts)
 
@@ -459,6 +462,7 @@
     return pl.pallas_call(
         zero_body,
         out_shape=[jax.ShapeDtypeStruct(s, BF) for s in shapes],
+        compiler_params=pltpu.CompilerParams(vmem_limit_bytes=8 * MIB),
         name="zeros",
     )()
 
@@ -520,6 +524,7 @@
             pltpu.SemaphoreType.DMA((CAP, 3)),
         ],
         input_output_aliases={10: 0, 11: 1, 12: 2},
+        compiler_params=pltpu.CompilerParams(vmem_limit_bytes=10 * MIB),
         name="unpack",
     )(mask, where, *downs, *pairs, *blanks)
 

time: 303 us -> 284 us (0.937)
  Pallas kernels: 57.9 us -> 43.9 us
  waiting for transfers between devices: 163 us -> 175 us
  other arithmetic: 15 us -> 4.07 us
  local copies, waits for them, and re-layouts: 14.6 us -> 5.89 us
  starting transfers between devices: 49.2 us -> 53.5 us
    ppermute x41, waiting for transfers between devices: 163 us -> 175 us  [send(): return lax.ppermute(v, ('row', 'col'), shift(axis, k))]
    convert_element_type x6, other arithmetic: 13.3 us -> 3.07 us  [add(): return total.astype(BF)]
    unnamed x88 -> x32, local copies, waits for them, and re-layouts: 13.3 us -> 5.56 us
    pallas_call x1, Pallas kernels: 7.48 us -> 2.03 us  [stage(): pl.pallas_call(stage_body, out_shape=jax.ShapeDtypeStruct((8 * CAP + 1, B...]
    ppermute x41, starting transfers between devices: 49.2 us -> 53.5 us  [send(): return lax.ppermute(v, ('row', 'col'), shift(axis, k))]
  transfers between devices with their start and end apart: 41 -> 41, of which waited for: 13 -> 17; matrix products, arithmetic and copies ran while one was open for 6% -> 2% of each run, Pallas kernels for 9% -> 8%
where the time goes in v2:
time: 284 us; the launch traced here: 283 us
  waiting for transfers between devices  175 us (62%)
  starting transfers between devices  53.5 us (19%)
  Pallas kernels  43.9 us (15%)
  local copies, waits for them, and re-layouts  5.89 us (2%)
  other arithmetic  4.07 us (1%)
    ppermute x41, waiting for transfers between devices, send(): return lax.ppermute(v, ('row', 'col'), shift(axis, k))  175 us
    ppermute x41, starting transfers between devices, send(): return lax.ppermute(v, ('row', 'col'), shift(axis, k))  53.5 us
    pallas_call x1, Pallas kernels, input_work(): pl.pallas_call(input_body, out_shape=part_shapes(256, BLK) + grad_shapes(...  11.5 us
    pallas_call x1, Pallas kernels, forward_work(): pl.pallas_call(forward_body, out_shape=part_shapes(256, BLK) + [jax.Shape...  9.41 us
    pallas_call x1, Pallas kernels, plan(): pl.pallas_call(plan_body, out_shape=jax.ShapeDtypeStruct((8, 128), jnp.in...  7.86 us
  transfers between devices with their start and end apart: 41, of which 17 were waited for; matrix products, arithmetic and copies ran while one was open for 2% of the time, Pallas kernels for 8%

profile of v2, /device:TPU:0, one launch (start us, length us, event | category | flops | bytes accessed | tf_op | source)
XLA Modules:
  0.0 283.4 jit_solution(14754916103580317145)
XLA Ops:
  0.7 1.5 copy-done
  2.2 1.5 copy-done.1
  3.7 1.5 copy-done.2
  5.2 0.8 copy-done.3
  6.0 2.4 pack.1.refs_0_
  8.5 2.1 collective-permute-start.6
  10.5 2.0 collective-permute-start.7
  12.7 1.4 collective-permute-start
  14.1 1.9 collective-permute-start.1
  16.0 1.8 collective-permute-start.2
  17.9 4.7 %collective-permute-done = bf16[4,256,128]{2,1,0:T(8,128)(2,1)S(1)} collective-permute-done((bf16[4,256,128]{2,1,0:T(8,128)(2,1)S(1)}, bf16[4,256,128]{2,1,0:T(8,128)(2,1)S(1)}, u32[]{:S(2)}, u32[]{:S(2)}) %collective-permute-start) | collective-permute-done | bytes 262176 | tf_op jit(solution)/shard_map/ppermute | solution.py:29
  22.6 0.7 collective-permute-done.1
  23.3 5.0 %collective-permute-start.21 = (bf16[4,256,128]{2,1,0:T(8,128)(2,1)S(1)}, bf16[4,256,128]{2,1,0:T(8,128)(2,1)S(1)}, u32[]{:S(2)}, u32[]{:S(2)}) collective-permute-start(bf16[4,256,128]{2,1,0:T(8,128)(2,1)S(1)} %pad_maximum_fusion.2), channel_id=1, source_target_pairs={{0,1},{1,2},{2,3},{3,0},{4,5},{5,6},{6,7},{7,4},{8,9},{9,10},{10,1... | collective-permute-start | bytes 786440 | tf_op jit(solution)/shard_map/ppermute | solution.py:29
  28.2 10.3 %collective-permute-done.6.refs_1_ = bf16[12,128,384]{2,1,0:T(8,128)(2,1)S(1)} collective-permute-done((bf16[12,128,384]{2,1,0:T(8,128)(2,1)S(1)}, bf16[12,128,384]{2,1,0:T(8,128)(2,1)S(1)}, u32[]{:S(2)}, u32[]{:S(2)}) %collective-permute-start.6) | collective-permute-done | bytes 1179680 | tf_op jit(solution)/shard_map/ppermute | solution.py:29
  38.5 3.0 %collective-permute-start.22 = (bf16[4,256,128]{2,1,0:T(8,128)(2,1)S(1)}, bf16[4,256,128]{2,1,0:T(8,128)(2,1)S(1)}, u32[]{:S(2)}, u32[]{:S(2)}) collective-permute-start(bf16[4,256,128]{2,1,0:T(8,128)(2,1)S(1)} %pad_maximum_fusion.2), channel_id=1, source_target_pairs={{0,3},{1,0},{2,1},{3,2},{4,7},{5,4},{6,5},{7,6},{8,11},{9,8},{10,9... | collective-permute-start | bytes 786440 | tf_op jit(solution)/shard_map/ppermute | solution.py:29
  41.5 0.6 collective-permute-start.23
  42.3 1.0 collective-permute-start.8
  43.4 2.3 collective-permute-start.9
  45.6 6.6 %collective-permute-done.22 = bf16[4,256,128]{2,1,0:T(8,128)(2,1)S(1)} collective-permute-done((bf16[4,256,128]{2,1,0:T(8,128)(2,1)S(1)}, bf16[4,256,128]{2,1,0:T(8,128)(2,1)S(1)}, u32[]{:S(2)}, u32[]{:S(2)}) %collective-permute-start.22) | collective-permute-done | bytes 262176 | tf_op jit(solution)/shard_map/ppermute | solution.py:29
  52.3 0.5 collective-permute-start.12
  53.0 1.3 collective-permute-start.3
  54.3 3.4 %collective-permute-done.8.refs_3_ = bf16[6,128,384]{2,1,0:T(8,128)(2,1)S(1)} collective-permute-done((bf16[6,128,384]{2,1,0:T(8,128)(2,1)S(1)}, bf16[6,128,384]{2,1,0:T(8,128)(2,1)S(1)}, u32[]{:S(2)}, u32[]{:S(2)}) %collective-permute-start.8) | collective-permute-done | bytes 589856 | tf_op jit(solution)/shard_map/ppermute | solution.py:29
  57.7 0.9 collective-permute-start.4
  58.6 2.0 collective-permute-start.5
  60.7 0.5 collective-permute-start.14
  61.3 7.9 %plan.1.table = s32[8,128]{1,0:T(8,128)S(1)} custom-call(s32[64,112]{1,0:T(8,128)S(1)} %copy-done.4, s32[4]{0:T(128)S(1)} %pad_add_fusion.where), custom_call_target="tpu_custom_call" | custom-call | tf_op jit(solution)/shard_map/plan/pallas_call | solution.py:163
  69.3 1.5 collective-permute-start.24
  70.9 1.8 collective-permute-start.25
  72.6 2.0 stage.1.refs_4_
  74.7 5.4 %collective-permute-done.3.refs_1_ = bf16[16,256,128]{2,1,0:T(8,128)(2,1)S(1)} collective-permute-done((bf16[16,256,128]{2,1,0:T(8,128)(2,1)S(1)}, bf16[16,256,128]{2,1,0:T(8,128)(2,1)S(1)}, u32[]{:S(2)}, u32[]{:S(2)}) %collective-permute-start.3) | collective-permute-done | bytes 1048608 | tf_op jit(solution)/shard_map/ppermute | solution.py:29
  80.0 3.0 %collective-permute-start.26 = (bf16[16,256,128]{2,1,0:T(8,128)(2,1)S(1)}, bf16[16,256,128]{2,1,0:T(8,128)(2,1)S(1)}, u32[]{:S(2)}, u32[]{:S(2)}) collective-permute-start(bf16[16,256,128]{2,1,0:T(8,128)(2,1)S(1)} %constant_dynamic-update-slice_fusion.7.refs_0_), channel_id=1, source_target_pairs={{0,8},{1,9},{2,10},{3,11},{4,12},{5,13},{6,14},{7,15},{8,0},{9,1},... | collective-permute-start | bytes 3145736 | tf_op jit(solution)/shard_map/ppermute | solution.py:29
  83.1 0.7 collective-permute-done.4.refs_2_
  83.7 20.0 %collective-permute-done.5.refs_3_ = bf16[16,256,128]{2,1,0:T(8,128)(2,1)S(1)} collective-permute-done((bf16[16,256,128]{2,1,0:T(8,128)(2,1)S(1)}, bf16[16,256,128]{2,1,0:T(8,128)(2,1)S(1)}, u32[]{:S(2)}, u32[]{:S(2)}) %collective-permute-start.5) | collective-permute-done | bytes 1048608 | tf_op jit(solution)/shard_map/ppermute | solution.py:29
  103.7 9.4 %forward.1 = (bf16[16,256,128]{2,1,0:T(8,128)(2,1)S(1)}, bf16[16,256,128]{2,1,0:T(8,128)(2,1)S(1)}, bf16[16,256,128]{2,1,0:T(8,128)(2,1)S(1)}, bf16[16,256,128]{...) custom-call(s32[8,128]{1,0:T(8,128)S(1)} %plan.1.table, ...), custom_call_target="tpu_custom_call" | custom-call | flops 45097156608 | bytes 20971520 | tf_op jit(solution)/shard_map/forward/pallas_call | solution.py:326
  113.1 4.6 %collective-permute-done.25.refs_2_ = bf16[16,256,128]{2,1,0:T(8,128)(2,1)S(1)} collective-permute-done((bf16[16,256,128]{2,1,0:T(8,128)(2,1)S(1)}, bf16[16,256,128]{2,1,0:T(8,128)(2,1)S(1)}, u32[]{:S(2)}, u32[]{:S(2)}) %collective-permute-start.25) | collective-permute-done | bytes 1048608 | tf_op jit(solution)/shard_map/ppermute | solution.py:29
  117.7 1.8 collective-permute-done.26.refs_3_
  119.5 11.5 %inputs.1 = (bf16[16,256,128]{2,1,0:T(8,128)(2,1)S(1)}, bf16[16,256,128]{2,1,0:T(8,128)(2,1)S(1)}, bf16[16,256,128]{2,1,0:T(8,128)(2,1)S(1)}, bf16[16,256,128]{2...) custom-call(s32[8,128]{1,0:T(8,128)S(1)} %plan.1.table, ...), custom_call_target="tpu_custom_call" | custom-call | flops 60129542144 | bytes 23068672 | tf_op jit(solution)/shard_map/inputs/pallas_call | solution.py:398
  131.1 4.9 %grads.1 = (bf16[12,128,256]{2,1,0:T(8,128)(2,1)S(1)}, bf16[12,128,256]{2,1,0:T(8,128)(2,1)S(1)}, bf16[12,128,256]{2,1,0:T(8,128)(2,1)S(1)}, bf16[12,128,256]{2,1,0:T(8,128)(2,1)S(1)}, bf16[48,128,256]{2,1,0:T(8,128)(2,1)S(1)}) custom-call(s32[8,128]{1,0:T(8,128)S(1)} %plan.1.table, bf16[7,256,256]{2,1,0:T(8,128)(2,1)S(1)} %get-tuple-element.47.gucot, ...), custom_call_target="tpu_custom_call" | custom-call | flops 30064771072 | bytes 10485760 | tf_op jit(solution)/shard_map/grads/pallas_call | solution.py:440
  136.3 1.3 collective-permute-start.17
  137.5 1.1 collective-permute-start.16
  138.7 2.1 collective-permute-start.15
  140.8 1.3 collective-permute-start.29
  142.0 21.9 %collective-permute-done.17 = bf16[16,256,128]{2,1,0:T(8,128)(2,1)S(1)} collective-permute-done((bf16[16,256,128]{2,1,0:T(8,128)(2,1)S(1)}, bf16[16,256,128]{2,1,0:T(8,128)(2,1)S(1)}, u32[]{:S(2)}, u32[]{:S(2)}) %collective-permute-start.17) | collective-permute-done | bytes 1048608 | tf_op jit(solution)/shard_map/ppermute | solution.py:29
  163.9 21.8 %collective-permute-done.16 = bf16[16,256,128]{2,1,0:T(8,128)(2,1)S(1)} collective-permute-done((bf16[16,256,128]{2,1,0:T(8,128)(2,1)S(1)}, bf16[16,256,128]{2,1,0:T(8,128)(2,1)S(1)}, u32[]{:S(2)}, u32[]{:S(2)}) %collective-permute-start.16) | collective-permute-done | bytes 1048608 | tf_op jit(solution)/shard_map/ppermute | solution.py:29
  185.8 0.8 collective-permute-start.27
  186.6 2.6 zeros.1
  189.1 0.4 add_convert_fusion.16
  189.6 1.1 collective-permute-start.20
  190.7 0.3 collective-permute-start.19
  191.0 20.8 %collective-permute-done.27 = bf16[16,256,128]{2,1,0:T(8,128)(2,1)S(1)} collective-permute-done((bf16[16,256,128]{2,1,0:T(8,128)(2,1)S(1)}, bf16[16,256,128]{2,1,0:T(8,128)(2,1)S(1)}, u32[]{:S(2)}, u32[]{:S(2)}) %collective-permute-start.27) | collective-permute-done | bytes 1048608 | tf_op jit(solution)/shard_map/ppermute | solution.py:29
  211.8 1.3 collective-permute-start.18
  213.1 0.4 add_convert_fusion.11
  213.5 1.9 collective-permute-start.32
  215.4 6.7 %collective-permute-done.18 = bf16[4,256,128]{2,1,0:T(8,128)(2,1)S(1)} collective-permute-done((bf16[4,256,128]{2,1,0:T(8,128)(2,1)S(1)}, bf16[4,256,128]{2,1,0:T(8,128)(2,1)S(1)}, u32[]{:S(2)}, u32[]{:S(2)}) %collective-permute-start.18) | collective-permute-done | bytes 262176 | tf_op jit(solution)/shard_map/ppermute | solution.py:29
  222.6 0.5 add_convert_fusion.4
  223.1 3.0 %collective-permute-start.34 = (bf16[12,128,128]{2,1,0:T(8,128)(2,1)S(1)}, bf16[12,128,128]{2,1,0:T(8,128)(2,1)S(1)}, u32[]{:S(2)}, u32[]{:S(2)}) collective-permute-start(bf16[12,128,128]{2,1,0:T(8,128)(2,1)S(1)} %get-tuple-element.71), channel_id=1, source_target_pairs={{0,96},{1,97},{2,98},{3,99},{4,100},{5,101},{6,102},{7,103},{8,104... | collective-permute-start | bytes 1179656 | tf_op jit(solution)/shard_map/ppermute | solution.py:29
  226.1 1.2 add_convert_fusion
  227.4 2.0 collective-permute-start.39
  229.8 2.1 collective-permute-start.35
  231.9 3.7 %collective-permute-done.34.refs_1_ = bf16[12,128,128]{2,1,0:T(8,128)(2,1)S(1)} collective-permute-done((bf16[12,128,128]{2,1,0:T(8,128)(2,1)S(1)}, bf16[12,128,128]{2,1,0:T(8,128)(2,1)S(1)}, u32[]{:S(2)}, u32[]{:S(2)}) %collective-permute-start.34) | collective-permute-done | bytes 393248 | tf_op jit(solution)/shard_map/ppermute | solution.py:29
  235.6 1.9 collective-permute-start.36
  237.6 0.9 pad_maximum_fusion.1
  238.4 41.6 %collective-permute-done.35.refs_2_ = bf16[12,128,128]{2,1,0:T(8,128)(2,1)S(1)} collective-permute-done((bf16[12,128,128]{2,1,0:T(8,128)(2,1)S(1)}, bf16[12,128,128]{2,1,0:T(8,128)(2,1)S(1)}, u32[]{:S(2)}, u32[]{:S(2)}) %collective-permute-start.35) | collective-permute-done | bytes 393248 | tf_op jit(solution)/shard_map/ppermute | solution.py:29
  280.1 3.1 %unpack.1 = (bf16[1024,896]{1,0:T(8,128)(2,1)}, bf16[1024,896]{1,0:T(8,128)(2,1)}, bf16[896,1024]{1,0:T(8,128)(2,1)}) custom-call(s32[64,112]{1,0:T(8,128)S(1)} %copy-done.5, s32[4]{0:T(128)S(1)} %copy-done.7, bf16[12,128,128]{2,1,0:T(8,128)(2,1)S(1)} %get-tuple-element.72.refs_0_, ...), custom_call_target="tpu_custom_call", output_to_operand_aliasing={{0}: (10, {}), {1}: (11, {}), {2}: (12, {})} | custom-call | tf_op jit(solution)/shard_map/unpack/pallas_call | solution.py:517
  (76 shorter events, 2.1 us)
Async XLA Ops:
  0.7 1.5 copy-start
  2.2 1.5 copy-start.1
  3.7 1.5 copy-start.2
  5.2 0.8 copy-start.3
  6.0 55.3 %copy-start.6 = (s32[4]{0:T(128)}, s32[4]{0:T(128)S(1)}, u32[]{:S(2)}) copy-start(s32[4]{0:T(128)S(1)} %pad_add_fusion.where) | copy-start | bytes 52
  6.0 6.6 %copy-start.8 = (bf16[256,512]{1,0:T(8,128)(2,1)S(1)}, bf16[256,512]{1,0:T(8,128)(2,1)}, u32[]{:S(2)}) copy-start(bf16[256,512]{1,0:T(8,128)(2,1)} %param.6) | copy-start | bytes 786436
  6.0 11.8 %copy-start.9 = (bf16[256,512]{1,0:T(8,128)(2,1)S(1)}, bf16[256,512]{1,0:T(8,128)(2,1)}, u32[]{:S(2)}) copy-start(bf16[256,512]{1,0:T(8,128)(2,1)} %param.7) | copy-start | bytes 786436
  8.5 30.0 %collective-permute-start.6 = (bf16[12,128,384]{2,1,0:T(8,128)(2,1)S(1)}, bf16[12,128,384]{2,1,0:T(8,128)(2,1)S(1)}, u32[]{:S(2)}, u32[]{:S(2)}) collective-permute-start(bf16[12,128,384]{2,1,0:T(8,128)(2,1)S(1)} %pack.1.refs_0_), channel_id=1, source_target_pairs={{0,32},{1,33},{2,34},{3,35},{4,36},{5,37},{6,38},{7,39},{8,40},{9,... | collective-permute-start | bytes 3538952 | tf_op jit(solution)/shard_map/ppermute | solution.py:29
  10.5 31.0 %collective-permute-start.7 = (bf16[12,128,384]{2,1,0:T(8,128)(2,1)S(1)}, bf16[12,128,384]{2,1,0:T(8,128)(2,1)S(1)}, u32[]{:S(2)}, u32[]{:S(2)}) collective-permute-start(bf16[12,128,384]{2,1,0:T(8,128)(2,1)S(1)} %pack.1.refs_0_), channel_id=1, source_target_pairs={{0,96},{1,97},{2,98},{3,99},{4,100},{5,101},{6,102},{7,103},{8,104... | collective-permute-start | bytes 3538952 | tf_op jit(solution)/shard_map/ppermute | solution.py:29
  12.7 9.9 %collective-permute-start = (bf16[4,256,128]{2,1,0:T(8,128)(2,1)S(1)}, bf16[4,256,128]{2,1,0:T(8,128)(2,1)S(1)}, u32[]{:S(2)}, u32[]{:S(2)}) collective-permute-start(bf16[4,256,128]{2,1,0:T(8,128)(2,1)S(1)} %pad_maximum_fusion), channel_id=1, source_target_pairs={{0,4},{1,5},{2,6},{3,7},{4,8},{5,9},{6,10},{7,11},{8,12},{9,13},{1... | collective-permute-start | bytes 786440 | tf_op jit(solution)/shard_map/ppermute | solution.py:29
  14.1 9.2 %collective-permute-start.1 = (bf16[4,256,128]{2,1,0:T(8,128)(2,1)S(1)}, bf16[4,256,128]{2,1,0:T(8,128)(2,1)S(1)}, u32[]{:S(2)}, u32[]{:S(2)}) collective-permute-start(bf16[4,256,128]{2,1,0:T(8,128)(2,1)S(1)} %pad_maximum_fusion), channel_id=1, source_target_pairs={{0,12},{1,13},{2,14},{3,15},{4,0},{5,1},{6,2},{7,3},{8,4},{9,5},{1... | collective-permute-start | bytes 786440 | tf_op jit(solution)/shard_map/ppermute | solution.py:29
  16.0 26.3 %collective-permute-start.2 = (bf16[4,256,128]{2,1,0:T(8,128)(2,1)S(1)}, bf16[4,256,128]{2,1,0:T(8,128)(2,1)S(1)}, u32[]{:S(2)}, u32[]{:S(2)}) collective-permute-start(bf16[4,256,128]{2,1,0:T(8,128)(2,1)S(1)} %pad_maximum_fusion), channel_id=1, source_target_pairs={{0,8},{1,9},{2,10},{3,11},{4,12},{5,13},{6,14},{7,15},{8,0},{9,1},... | collective-permute-start | bytes 786440 | tf_op jit(solution)/shard_map/ppermute | solution.py:29
  22.6 30.3 %collective-permute-start.10 = (bf16[12,128,384]{2,1,0:T(8,128)(2,1)S(1)}, bf16[12,128,384]{2,1,0:T(8,128)(2,1)S(1)}, u32[]{:S(2)}, u32[]{:S(2)}) collective-permute-start(bf16[12,128,384]{2,1,0:T(8,128)(2,1)S(1)} %pack.1.refs_0_), channel_id=1, source_target_pairs={{0,16},{1,17},{2,18},{3,19},{4,20},{5,21},{6,22},{7,23},{8,24},{9,... | collective-permute-start | bytes 3538952 | tf_op jit(solution)/shard_map/ppermute | solution.py:29
  23.3 20.1 %collective-permute-start.21 = (bf16[4,256,128]{2,1,0:T(8,128)(2,1)S(1)}, bf16[4,256,128]{2,1,0:T(8,128)(2,1)S(1)}, u32[]{:S(2)}, u32[]{:S(2)}) collective-permute-start(bf16[4,256,128]{2,1,0:T(8,128)(2,1)S(1)} %pad_maximum_fusion.2), channel_id=1, source_target_pairs={{0,1},{1,2},{2,3},{3,0},{4,5},{5,6},{6,7},{7,4},{8,9},{9,10},{10,1... | collective-permute-start | bytes 786440 | tf_op jit(solution)/shard_map/ppermute | solution.py:29
  38.5 13.8 %collective-permute-start.22 = (bf16[4,256,128]{2,1,0:T(8,128)(2,1)S(1)}, bf16[4,256,128]{2,1,0:T(8,128)(2,1)S(1)}, u32[]{:S(2)}, u32[]{:S(2)}) collective-permute-start(bf16[4,256,128]{2,1,0:T(8,128)(2,1)S(1)} %pad_maximum_fusion.2), channel_id=1, source_target_pairs={{0,3},{1,0},{2,1},{3,2},{4,7},{5,4},{6,5},{7,6},{8,11},{9,8},{10,9... | collective-permute-start | bytes 786440 | tf_op jit(solution)/shard_map/ppermute | solution.py:29
  41.5 10.8 %collective-permute-start.23 = (bf16[4,256,128]{2,1,0:T(8,128)(2,1)S(1)}, bf16[4,256,128]{2,1,0:T(8,128)(2,1)S(1)}, u32[]{:S(2)}, u32[]{:S(2)}) collective-permute-start(bf16[4,256,128]{2,1,0:T(8,128)(2,1)S(1)} %pad_maximum_fusion.2), channel_id=1, source_target_pairs={{0,2},{1,3},{2,0},{3,1},{4,6},{5,7},{6,4},{7,5},{8,10},{9,11},{10,... | collective-permute-start | bytes 786440 | tf_op jit(solution)/shard_map/ppermute | solution.py:29
  42.2 19.0 %copy-start.4 = (s32[64,112]{1,0:T(8,128)S(1)}, s32[64,112]{1,0:T(8,128)}, u32[]{:S(2)}) copy-start(s32[64,112]{1,0:T(8,128)} %mask.5) | copy-start | bytes 86020
  42.3 15.4 %collective-permute-start.8 = (bf16[6,128,384]{2,1,0:T(8,128)(2,1)S(1)}, bf16[6,128,384]{2,1,0:T(8,128)(2,1)S(1)}, u32[]{:S(2)}, u32[]{:S(2)}) collective-permute-start(bf16[6,128,384]{2,1,0:T(8,128)(2,1)S(1)} %slice.232), channel_id=1, source_target_pairs={{0,32},{1,33},{2,34},{3,35},{4,36},{5,37},{6,38},{7,39},{8,40},{9,... | collective-permute-start | bytes 1769480 | tf_op jit(solution)/shard_map/ppermute | solution.py:29
  43.4 15.2 %collective-permute-start.9 = (bf16[6,128,384]{2,1,0:T(8,128)(2,1)S(1)}, bf16[6,128,384]{2,1,0:T(8,128)(2,1)S(1)}, u32[]{:S(2)}, u32[]{:S(2)}) collective-permute-start(bf16[6,128,384]{2,1,0:T(8,128)(2,1)S(1)} %slice.233), channel_id=1, source_target_pairs={{0,96},{1,97},{2,98},{3,99},{4,100},{5,101},{6,102},{7,103},{8,104... | collective-permute-start | bytes 1769480 | tf_op jit(solution)/shard_map/ppermute | solution.py:29
  52.3 8.4 %collective-permute-start.11 = (bf16[12,128,384]{2,1,0:T(8,128)(2,1)S(1)}, bf16[12,128,384]{2,1,0:T(8,128)(2,1)S(1)}, u32[]{:S(2)}, u32[]{:S(2)}) collective-permute-start(bf16[12,128,384]{2,1,0:T(8,128)(2,1)S(1)} %collective-permute-done.6.refs_1_), channel_id=1, source_target_pairs={{0,16},{1,17},{2,18},{3,19},{4,20},{5,21},{6,22},{7,23},{8,24},{9,... | collective-permute-start | bytes 3538952 | tf_op jit(solution)/shard_map/ppermute | solution.py:29
  52.3 8.5 %collective-permute-start.12 = (bf16[12,128,384]{2,1,0:T(8,128)(2,1)S(1)}, bf16[12,128,384]{2,1,0:T(8,128)(2,1)S(1)}, u32[]{:S(2)}, u32[]{:S(2)}) collective-permute-start(bf16[12,128,384]{2,1,0:T(8,128)(2,1)S(1)} %collective-permute-done.7.refs_2_), channel_id=1, source_target_pairs={{0,16},{1,17},{2,18},{3,19},{4,20},{5,21},{6,22},{7,23},{8,24},{9,... | collective-permute-start | bytes 3538952 | tf_op jit(solution)/shard_map/ppermute | solution.py:29
  53.0 27.1 %collective-permute-start.3 = (bf16[16,256,128]{2,1,0:T(8,128)(2,1)S(1)}, bf16[16,256,128]{2,1,0:T(8,128)(2,1)S(1)}, u32[]{:S(2)}, u32[]{:S(2)}) collective-permute-start(bf16[16,256,128]{2,1,0:T(8,128)(2,1)S(1)} %constant_dynamic-update-slice_fusion.refs_0_), channel_id=1, source_target_pairs={{0,1},{1,2},{2,3},{3,0},{4,5},{5,6},{6,7},{7,4},{8,9},{9,10},{10,1... | collective-permute-start | bytes 3145736 | tf_op jit(solution)/shard_map/ppermute | solution.py:29
  57.7 26.0 %collective-permute-start.4 = (bf16[16,256,128]{2,1,0:T(8,128)(2,1)S(1)}, bf16[16,256,128]{2,1,0:T(8,128)(2,1)S(1)}, u32[]{:S(2)}, u32[]{:S(2)}) collective-permute-start(bf16[16,256,128]{2,1,0:T(8,128)(2,1)S(1)} %constant_dynamic-update-slice_fusion.refs_0_), channel_id=1, source_target_pairs={{0,3},{1,0},{2,1},{3,2},{4,7},{5,4},{6,5},{7,6},{8,11},{9,8},{10,9... | collective-permute-start | bytes 3145736 | tf_op jit(solution)/shard_map/ppermute | solution.py:29
  58.6 45.1 %collective-permute-start.5 = (bf16[16,256,128]{2,1,0:T(8,128)(2,1)S(1)}, bf16[16,256,128]{2,1,0:T(8,128)(2,1)S(1)}, u32[]{:S(2)}, u32[]{:S(2)}) collective-permute-start(bf16[16,256,128]{2,1,0:T(8,128)(2,1)S(1)} %constant_dynamic-update-slice_fusion.refs_0_), channel_id=1, source_target_pairs={{0,2},{1,3},{2,0},{3,1},{4,6},{5,7},{6,4},{7,5},{8,10},{9,11},{10,... | collective-permute-start | bytes 3145736 | tf_op jit(solution)/shard_map/ppermute | solution.py:29
  60.6 8.7 %collective-permute-start.13 = (bf16[6,128,384]{2,1,0:T(8,128)(2,1)S(1)}, bf16[6,128,384]{2,1,0:T(8,128)(2,1)S(1)}, u32[]{:S(2)}, u32[]{:S(2)}) collective-permute-start(bf16[6,128,384]{2,1,0:T(8,128)(2,1)S(1)} %collective-permute-done.8.refs_3_), channel_id=1, source_target_pairs={{0,16},{1,17},{2,18},{3,19},{4,20},{5,21},{6,22},{7,23},{8,24},{9,... | collective-permute-start | bytes 1769480 | tf_op jit(solution)/shard_map/ppermute | solution.py:29
  60.7 10.1 %collective-permute-start.14 = (bf16[6,128,384]{2,1,0:T(8,128)(2,1)S(1)}, bf16[6,128,384]{2,1,0:T(8,128)(2,1)S(1)}, u32[]{:S(2)}, u32[]{:S(2)}) collective-permute-start(bf16[6,128,384]{2,1,0:T(8,128)(2,1)S(1)} %collective-permute-done.9.refs_4_), channel_id=1, source_target_pairs={{0,16},{1,17},{2,18},{3,19},{4,20},{5,21},{6,22},{7,23},{8,24},{9,... | collective-permute-start | bytes 1769480 | tf_op jit(solution)/shard_map/ppermute | solution.py:29
  69.3 43.8 %collective-permute-start.24 = (bf16[16,256,128]{2,1,0:T(8,128)(2,1)S(1)}, bf16[16,256,128]{2,1,0:T(8,128)(2,1)S(1)}, u32[]{:S(2)}, u32[]{:S(2)}) collective-permute-start(bf16[16,256,128]{2,1,0:T(8,128)(2,1)S(1)} %constant_dynamic-update-slice_fusion.7.refs_0_), channel_id=1, source_target_pairs={{0,4},{1,5},{2,6},{3,7},{4,8},{5,9},{6,10},{7,11},{8,12},{9,13},{1... | collective-permute-start | bytes 3145736 | tf_op jit(solution)/shard_map/ppermute | solution.py:29
  70.9 46.9 %collective-permute-start.25 = (bf16[16,256,128]{2,1,0:T(8,128)(2,1)S(1)}, bf16[16,256,128]{2,1,0:T(8,128)(2,1)S(1)}, u32[]{:S(2)}, u32[]{:S(2)}) collective-permute-start(bf16[16,256,128]{2,1,0:T(8,128)(2,1)S(1)} %constant_dynamic-update-slice_fusion.7.refs_0_), channel_id=1, source_target_pairs={{0,12},{1,13},{2,14},{3,15},{4,0},{5,1},{6,2},{7,3},{8,4},{9,5},{1... | collective-permute-start | bytes 3145736 | tf_op jit(solution)/shard_map/ppermute | solution.py:29
  80.0 39.5 %collective-permute-start.26 = (bf16[16,256,128]{2,1,0:T(8,128)(2,1)S(1)}, bf16[16,256,128]{2,1,0:T(8,128)(2,1)S(1)}, u32[]{:S(2)}, u32[]{:S(2)}) collective-permute-start(bf16[16,256,128]{2,1,0:T(8,128)(2,1)S(1)} %constant_dynamic-update-slice_fusion.7.refs_0_), channel_id=1, source_target_pairs={{0,8},{1,9},{2,10},{3,11},{4,12},{5,13},{6,14},{7,15},{8,0},{9,1},... | collective-permute-start | bytes 3145736 | tf_op jit(solution)/shard_map/ppermute | solution.py:29
  136.0 90.1 %collective-permute-start.37 = (bf16[48,128,256]{2,1,0:T(8,128)(2,1)S(1)}, bf16[48,128,256]{2,1,0:T(8,128)(2,1)S(1)}, u32[]{:S(2)}, u32[]{:S(2)}) collective-permute-start(bf16[48,128,256]{2,1,0:T(8,128)(2,1)S(1)} %get-tuple-element.49), channel_id=1, source_target_pairs={{0,16},{1,17},{2,18},{3,19},{4,20},{5,21},{6,22},{7,23},{8,24},{9,... | collective-permute-start | bytes 9437192 | tf_op jit(solution)/shard_map/ppermute | solution.py:29
  136.3 27.7 %collective-permute-start.17 = (bf16[16,256,128]{2,1,0:T(8,128)(2,1)S(1)}, bf16[16,256,128]{2,1,0:T(8,128)(2,1)S(1)}, u32[]{:S(2)}, u32[]{:S(2)}) collective-permute-start(bf16[16,256,128]{2,1,0:T(8,128)(2,1)S(1)} %get-tuple-element.35), channel_id=1, source_target_pairs={{0,2},{1,3},{2,0},{3,1},{4,6},{5,7},{6,4},{7,5},{8,10},{9,11},{10,... | collective-permute-start | bytes 3145736 | tf_op jit(solution)/shard_map/ppermute | solution.py:29
  137.5 48.3 %collective-permute-start.16 = (bf16[16,256,128]{2,1,0:T(8,128)(2,1)S(1)}, bf16[16,256,128]{2,1,0:T(8,128)(2,1)S(1)}, u32[]{:S(2)}, u32[]{:S(2)}) collective-permute-start(bf16[16,256,128]{2,1,0:T(8,128)(2,1)S(1)} %get-tuple-element.34), channel_id=1, source_target_pairs={{0,1},{1,2},{2,3},{3,0},{4,5},{5,6},{6,7},{7,4},{8,9},{9,10},{10,1... | collective-permute-start | bytes 3145736 | tf_op jit(solution)/shard_map/ppermute | solution.py:29
  138.7 47.9 %collective-permute-start.15 = (bf16[16,256,128]{2,1,0:T(8,128)(2,1)S(1)}, bf16[16,256,128]{2,1,0:T(8,128)(2,1)S(1)}, u32[]{:S(2)}, u32[]{:S(2)}) collective-permute-start(bf16[16,256,128]{2,1,0:T(8,128)(2,1)S(1)} %get-tuple-element.33), channel_id=1, source_target_pairs={{0,3},{1,0},{2,1},{3,2},{4,7},{5,4},{6,5},{7,6},{8,11},{9,8},{10,9... | collective-permute-start | bytes 3145736 | tf_op jit(solution)/shard_map/ppermute | solution.py:29
  140.8 48.8 %collective-permute-start.29 = (bf16[16,256,128]{2,1,0:T(8,128)(2,1)S(1)}, bf16[16,256,128]{2,1,0:T(8,128)(2,1)S(1)}, u32[]{:S(2)}, u32[]{:S(2)}) collective-permute-start(bf16[16,256,128]{2,1,0:T(8,128)(2,1)S(1)} %get-tuple-element.41), channel_id=1, source_target_pairs={{0,8},{1,9},{2,10},{3,11},{4,12},{5,13},{6,14},{7,15},{8,0},{9,1},... | collective-permute-start | bytes 3145736 | tf_op jit(solution)/shard_map/ppermute | solution.py:29
  163.9 26.8 %collective-permute-start.28 = (bf16[16,256,128]{2,1,0:T(8,128)(2,1)S(1)}, bf16[16,256,128]{2,1,0:T(8,128)(2,1)S(1)}, u32[]{:S(2)}, u32[]{:S(2)}) collective-permute-start(bf16[16,256,128]{2,1,0:T(8,128)(2,1)S(1)} %get-tuple-element.40), channel_id=1, source_target_pairs={{0,4},{1,5},{2,6},{3,7},{4,8},{5,9},{6,10},{7,11},{8,12},{9,13},{1... | collective-permute-start | bytes 3145736 | tf_op jit(solution)/shard_map/ppermute | solution.py:29
  185.8 26.0 %collective-permute-start.27 = (bf16[16,256,128]{2,1,0:T(8,128)(2,1)S(1)}, bf16[16,256,128]{2,1,0:T(8,128)(2,1)S(1)}, u32[]{:S(2)}, u32[]{:S(2)}) collective-permute-start(bf16[16,256,128]{2,1,0:T(8,128)(2,1)S(1)} %get-tuple-element.39), channel_id=1, source_target_pairs={{0,12},{1,13},{2,14},{3,15},{4,0},{5,1},{6,2},{7,3},{8,4},{9,5},{1... | collective-permute-start | bytes 3145736 | tf_op jit(solution)/shard_map/ppermute | solution.py:29
  186.6 36.0 %collective-permute-start.33 = (bf16[48,128,128]{2,1,0:T(8,128)(2,1)S(1)}, bf16[48,128,128]{2,1,0:T(8,128)(2,1)S(1)}, u32[]{:S(2)}, u32[]{:S(2)}) collective-permute-start(bf16[48,128,128]{2,1,0:T(8,128)(2,1)S(1)} %get-tuple-element.43), channel_id=1, source_target_pairs={{0,16},{1,17},{2,18},{3,19},{4,20},{5,21},{6,22},{7,23},{8,24},{9,... | collective-permute-start | bytes 4718600 | tf_op jit(solution)/shard_map/ppermute | solution.py:29
  189.6 24.0 %collective-permute-start.20 = (bf16[4,256,128]{2,1,0:T(8,128)(2,1)S(1)}, bf16[4,256,128]{2,1,0:T(8,128)(2,1)S(1)}, u32[]{:S(2)}, u32[]{:S(2)}) collective-permute-start(bf16[4,256,128]{2,1,0:T(8,128)(2,1)S(1)} %get-tuple-element.63), channel_id=1, source_target_pairs={{0,8},{1,9},{2,10},{3,11},{4,12},{5,13},{6,14},{7,15},{8,0},{9,1},... | collective-permute-start | bytes 786440 | tf_op jit(solution)/shard_map/ppermute | solution.py:29
  190.7 24.7 %collective-permute-start.19 = (bf16[4,256,128]{2,1,0:T(8,128)(2,1)S(1)}, bf16[4,256,128]{2,1,0:T(8,128)(2,1)S(1)}, u32[]{:S(2)}, u32[]{:S(2)}) collective-permute-start(bf16[4,256,128]{2,1,0:T(8,128)(2,1)S(1)} %get-tuple-element.64), channel_id=1, source_target_pairs={{0,4},{1,5},{2,6},{3,7},{4,8},{5,9},{6,10},{7,11},{8,12},{9,13},{1... | collective-permute-start | bytes 786440 | tf_op jit(solution)/shard_map/ppermute | solution.py:29
  211.8 10.3 %collective-permute-start.18 = (bf16[4,256,128]{2,1,0:T(8,128)(2,1)S(1)}, bf16[4,256,128]{2,1,0:T(8,128)(2,1)S(1)}, u32[]{:S(2)}, u32[]{:S(2)}) collective-permute-start(bf16[4,256,128]{2,1,0:T(8,128)(2,1)S(1)} %get-tuple-element.62), channel_id=1, source_target_pairs={{0,12},{1,13},{2,14},{3,15},{4,0},{5,1},{6,2},{7,3},{8,4},{9,5},{1... | collective-permute-start | bytes 786440 | tf_op jit(solution)/shard_map/ppermute | solution.py:29
  213.5 13.9 %collective-permute-start.32 = (bf16[4,256,128]{2,1,0:T(8,128)(2,1)S(1)}, bf16[4,256,128]{2,1,0:T(8,128)(2,1)S(1)}, u32[]{:S(2)}, u32[]{:S(2)}) collective-permute-start(bf16[4,256,128]{2,1,0:T(8,128)(2,1)S(1)} %get-tuple-element.60), channel_id=1, source_target_pairs={{0,2},{1,3},{2,0},{3,1},{4,6},{5,7},{6,4},{7,5},{8,10},{9,11},{10,... | collective-permute-start | bytes 786440 | tf_op jit(solution)/shard_map/ppermute | solution.py:29
  215.4 14.0 %collective-permute-start.31 = (bf16[4,256,128]{2,1,0:T(8,128)(2,1)S(1)}, bf16[4,256,128]{2,1,0:T(8,128)(2,1)S(1)}, u32[]{:S(2)}, u32[]{:S(2)}) collective-permute-start(bf16[4,256,128]{2,1,0:T(8,128)(2,1)S(1)} %get-tuple-element.61), channel_id=1, source_target_pairs={{0,1},{1,2},{2,3},{3,0},{4,5},{5,6},{6,7},{7,4},{8,9},{9,10},{10,1... | collective-permute-start | bytes 786440 | tf_op jit(solution)/shard_map/ppermute | solution.py:29
  222.2 7.4 %collective-permute-start.30 = (bf16[4,256,128]{2,1,0:T(8,128)(2,1)S(1)}, bf16[4,256,128]{2,1,0:T(8,128)(2,1)S(1)}, u32[]{:S(2)}, u32[]{:S(2)}) collective-permute-start(bf16[4,256,128]{2,1,0:T(8,128)(2,1)S(1)} %get-tuple-element.59), channel_id=1, source_target_pairs={{0,3},{1,0},{2,1},{3,2},{4,7},{5,4},{6,5},{7,6},{8,11},{9,8},{10,9... | collective-permute-start | bytes 786440 | tf_op jit(solution)/shard_map/ppermute | solution.py:29
  223.1 12.5 %collective-permute-start.34 = (bf16[12,128,128]{2,1,0:T(8,128)(2,1)S(1)}, bf16[12,128,128]{2,1,0:T(8,128)(2,1)S(1)}, u32[]{:S(2)}, u32[]{:S(2)}) collective-permute-start(bf16[12,128,128]{2,1,0:T(8,128)(2,1)S(1)} %get-tuple-element.71), channel_id=1, source_target_pairs={{0,96},{1,97},{2,98},{3,99},{4,100},{5,101},{6,102},{7,103},{8,104... | collective-permute-start | bytes 1179656 | tf_op jit(solution)/shard_map/ppermute | solution.py:29
  227.3 52.7 %collective-permute-start.38 = (bf16[12,128,256]{2,1,0:T(8,128)(2,1)S(1)}, bf16[12,128,256]{2,1,0:T(8,128)(2,1)S(1)}, u32[]{:S(2)}, u32[]{:S(2)}) collective-permute-start(bf16[12,128,256]{2,1,0:T(8,128)(2,1)S(1)} %get-tuple-element.67), channel_id=1, source_target_pairs={{0,96},{1,97},{2,98},{3,99},{4,100},{5,101},{6,102},{7,103},{8,104... | collective-permute-start | bytes 2359304 | tf_op jit(solution)/shard_map/ppermute | solution.py:29
  227.4 52.6 %collective-permute-start.39 = (bf16[12,128,256]{2,1,0:T(8,128)(2,1)S(1)}, bf16[12,128,256]{2,1,0:T(8,128)(2,1)S(1)}, u32[]{:S(2)}, u32[]{:S(2)}) collective-permute-start(bf16[12,128,256]{2,1,0:T(8,128)(2,1)S(1)} %get-tuple-element.66), channel_id=1, source_target_pairs={{0,32},{1,33},{2,34},{3,35},{4,36},{5,37},{6,38},{7,39},{8,40},{9,... | collective-permute-start | bytes 2359304 | tf_op jit(solution)/shard_map/ppermute | solution.py:29
  229.4 50.6 %collective-permute-start.40 = (bf16[12,128,256]{2,1,0:T(8,128)(2,1)S(1)}, bf16[12,128,256]{2,1,0:T(8,128)(2,1)S(1)}, u32[]{:S(2)}, u32[]{:S(2)}) collective-permute-start(bf16[12,128,256]{2,1,0:T(8,128)(2,1)S(1)} %get-tuple-element.65), channel_id=1, source_target_pairs={{0,64},{1,65},{2,66},{3,67},{4,68},{5,69},{6,70},{7,71},{8,72},{9,... | collective-permute-start | bytes 2359304 | tf_op jit(solution)/shard_map/ppermute | solution.py:29
  229.8 50.3 %copy-start.5 = (s32[64,112]{1,0:T(8,128)S(1)}, s32[64,112]{1,0:T(8,128)}, u32[]{:S(2)}) copy-start(s32[64,112]{1,0:T(8,128)} %mask.5) | copy-start | bytes 86020
  229.8 50.2 %copy-start.7 = (s32[4]{0:T(128)S(1)}, s32[4]{0:T(128)}, u32[]{:S(2)}) copy-start(s32[4]{0:T(128)} %copy-done.6) | copy-start | bytes 52
  229.8 50.2 %collective-permute-start.35 = (bf16[12,128,128]{2,1,0:T(8,128)(2,1)S(1)}, bf16[12,128,128]{2,1,0:T(8,128)(2,1)S(1)}, u32[]{:S(2)}, u32[]{:S(2)}) collective-permute-start(bf16[12,128,128]{2,1,0:T(8,128)(2,1)S(1)} %get-tuple-element.70), channel_id=1, source_target_pairs={{0,32},{1,33},{2,34},{3,35},{4,36},{5,37},{6,38},{7,39},{8,40},{9,... | collective-permute-start | bytes 1179656 | tf_op jit(solution)/shard_map/ppermute | solution.py:29
  235.6 44.4 %collective-permute-start.36 = (bf16[12,128,128]{2,1,0:T(8,128)(2,1)S(1)}, bf16[12,128,128]{2,1,0:T(8,128)(2,1)S(1)}, u32[]{:S(2)}, u32[]{:S(2)}) collective-permute-start(bf16[12,128,128]{2,1,0:T(8,128)(2,1)S(1)} %get-tuple-element.69), channel_id=1, source_target_pairs={{0,64},{1,65},{2,66},{3,67},{4,68},{5,69},{6,70},{7,71},{8,72},{9,... | collective-permute-start | bytes 1179656 | tf_op jit(solution)/shard_map/ppermute | solution.py:29
